TPU v7x, 128 devices: a whole 4x4x4 slice. The times are simulated.
128 devices in a mesh: dp: 4 (over z), expert: 32 (over y, x, core).
Axes of the slice: x: 4, y: 4, z: 4, core: 2. Of those that a mesh axis runs over, the one named last changes fastest.
Arguments:
- tokens: bfloat16 [16384, 2048], P(('dp', 'expert')), may hold values from -6 to 6
- out_grad: bfloat16 [16384, 2048], P(('dp', 'expert')), may hold values from -6 to 6
- gate_saved: bfloat16 [16384, 6, 1408], P(('dp', 'expert')), may hold values from -6 to 6
- probs: float32 [16384, 6], P(('dp', 'expert')), may hold values from 0.1 to 1
- expert_ids: int32 [16384, 6], P(('dp', 'expert')), may hold values from 0 to 31, all different within a row; in each aligned block of 128 rows (0 to 127, 128 to 255, ...) at most 48 rows name the same one
- w_gate: bfloat16 [32, 2048, 1408], P('expert'), may hold values from -0.125 to 0.125
- w_up: bfloat16 [32, 2048, 1408], P('expert'), may hold values from -0.125 to 0.125
- w_down: bfloat16 [32, 1408, 2048], P('expert'), may hold values from -0.15625 to 0.15625
Outputs:
- input_grad: bfloat16 [16384, 2048], P(('dp', 'expert'))
- grad_gate: bfloat16 [32, 2048, 1408], P('expert', 'dp')
- grad_up: bfloat16 [32, 2048, 1408], P('expert', 'dp')
- grad_down: bfloat16 [32, 1408, 2048], P('expert', 'dp')
Inputs may be any that keep to these rules, and one draw needn't show every extreme that they name: `expert_ids`: each token names 6 different experts. Among the 128 tokens of one aligned block (the tokens of one device) no expert is named more than 48 times, and in some block some expert is named exactly 48 times.
All inputs are finite; a program needn't handle non-finite values.
Results may differ from a plain program's by a relative error of at most 0.013.
Values may be sent and summed in bfloat16 or wider, within the bound.
A program may use at most 192 MiB of HBM per device.

v0:
```python
import jax
import jax.numpy as jnp
from jax import lax
from jax.sharding import PartitionSpec as P

grad_scale = 0.0625


def route_math(rows_in, routed_rows, gate_rows, gate_mat, up_mat, down_mat):
    contract_cols = (((1,), (1,)), ((), ()))
    up_act = jnp.dot(rows_in, up_mat, preferred_element_type=jnp.float32)
    gate_val = gate_rows.astype(jnp.float32)
    gate_sig = jax.nn.sigmoid(gate_val)
    gate_act = gate_val * gate_sig
    hidden_act = (gate_act * up_act).astype(jnp.bfloat16)
    hidden_grad = lax.dot_general(
        routed_rows, down_mat, contract_cols, preferred_element_type=jnp.float32
    )
    up_grad = (hidden_grad * gate_act).astype(jnp.bfloat16)
    gate_grad = (hidden_grad * up_act * gate_sig * (1.0 + gate_val * (1.0 - gate_sig))).astype(
        jnp.bfloat16
    )
    input_part = (
        lax.dot_general(gate_grad, gate_mat, contract_cols, preferred_element_type=jnp.float32)
        + lax.dot_general(up_grad, up_mat, contract_cols, preferred_element_type=jnp.float32)
    ).astype(jnp.bfloat16)
    return (input_part, gate_grad, up_grad, hidden_act)


def weight_terms(rows_in, routed_rows, gate_grad, up_grad, hidden_act):
    contract_rows = (((0,), (0,)), ((), ()))
    both_grads = jnp.concatenate([gate_grad, up_grad], axis=1)
    term_gate_up = lax.dot_general(
        rows_in, both_grads, contract_rows, preferred_element_type=jnp.float32
    )
    term_down = lax.dot_general(
        hidden_act, routed_rows, contract_rows, preferred_element_type=jnp.float32
    )
    return (term_gate_up, term_down)


def local(tokens, out_grad, gate_saved, probs, expert_ids, w_gate, w_up, w_down):
    n_peers = lax.axis_size("expert")
    tok_rows, model_width = tokens.shape
    top_k = expert_ids.shape[1]
    hidden_width = w_up.shape[2]
    slot_cap = min(tok_rows, 2 * tok_rows * top_k // n_peers)
    n_routes = tok_rows * top_k
    n_slots = n_peers * slot_cap
    row_block = 256
    padded_rows = -(-n_slots // row_block) * row_block
    flat_ids = expert_ids.reshape(n_routes)
    onehot = (flat_ids[:, None] == jnp.arange(n_peers, dtype=jnp.int32)[None, :]).astype(jnp.int32)
    slot_rank = jnp.sum((jnp.cumsum(onehot, axis=0) - 1) * onehot, axis=1)
    slot_of_route = flat_ids * slot_cap + slot_rank
    route_of_slot = (
        jnp.full((n_slots,), n_routes, jnp.int32)
        .at[slot_of_route]
        .set(jnp.arange(n_routes, dtype=jnp.int32))
    )
    used_slot = route_of_slot < n_routes
    safe_route = jnp.minimum(route_of_slot, n_routes - 1)
    token_of_slot = safe_route // top_k
    scaled = probs.reshape(n_routes)[safe_route][:, None] * out_grad[token_of_slot].astype(
        jnp.float32
    )
    send_grad = (
        jnp.where(used_slot[:, None], scaled, 0.0)
        .astype(jnp.bfloat16)
        .reshape(n_peers, slot_cap, model_width)
    )
    send_rows = jnp.where(used_slot[:, None], tokens[token_of_slot], 0).reshape(
        n_peers, slot_cap, model_width
    )
    send_gate = jnp.where(
        used_slot[:, None], gate_saved.reshape(n_routes, hidden_width)[safe_route], 0
    ).reshape(n_peers, slot_cap, hidden_width)
    gate_mat = w_gate[0]
    up_mat = w_up[0]
    down_mat = w_down[0]
    recv_rows, recv_grad, recv_gate = (
        lax.all_to_all(send_rows, "expert", split_axis=0, concat_axis=0, tiled=True),
        lax.all_to_all(send_grad, "expert", split_axis=0, concat_axis=0, tiled=True),
        lax.all_to_all(send_gate, "expert", split_axis=0, concat_axis=0, tiled=True),
    )
    recv_rows = recv_rows.reshape(n_slots, model_width)
    recv_grad = recv_grad.reshape(n_slots, model_width)
    recv_gate = recv_gate.reshape(n_slots, hidden_width)
    live_rows = jnp.any(recv_grad != 0, axis=1)
    dense_pos = jnp.where(live_rows, jnp.cumsum(live_rows.astype(jnp.int32)) - 1, padded_rows)
    n_live = jnp.sum(live_rows.astype(jnp.int32))
    dense_rows = (
        jnp.zeros((padded_rows, model_width), jnp.bfloat16)
        .at[dense_pos]
        .set(recv_rows, mode="drop")
    )
    dense_grad = (
        jnp.zeros((padded_rows, model_width), jnp.bfloat16)
        .at[dense_pos]
        .set(recv_grad, mode="drop")
    )
    dense_gate = (
        jnp.zeros((padded_rows, hidden_width), jnp.bfloat16)
        .at[dense_pos]
        .set(recv_gate, mode="drop")
    )
    n_blocks = (n_live + row_block - 1) // row_block

    def block_step(block_index, state):
        dense_out, acc_gate_up, acc_down = state
        first_row = block_index * row_block
        rows_in = lax.dynamic_slice_in_dim(dense_rows, first_row, row_block, 0)
        routed_rows = lax.dynamic_slice_in_dim(dense_grad, first_row, row_block, 0)
        gate_rows = lax.dynamic_slice_in_dim(dense_gate, first_row, row_block, 0)
        input_part, gate_grad, up_grad, hidden_act = route_math(
            rows_in, routed_rows, gate_rows, gate_mat, up_mat, down_mat
        )
        term_gate_up, term_down = weight_terms(rows_in, routed_rows, gate_grad, up_grad, hidden_act)
        dense_out = lax.dynamic_update_slice_in_dim(dense_out, input_part, first_row, 0)
        return (dense_out, acc_gate_up + term_gate_up, acc_down + term_down)

    start_state = (
        jnp.zeros((padded_rows, model_width), jnp.bfloat16),
        jnp.zeros((model_width, 2 * hidden_width), jnp.float32),
        jnp.zeros((hidden_width, model_width), jnp.float32),
    )
    dense_out, sum_gate_up, sum_down = lax.fori_loop(0, n_blocks, block_step, start_state)
    back_slots = jnp.where(
        live_rows[:, None], dense_out[jnp.minimum(dense_pos, padded_rows - 1)], 0
    )
    back_slots = back_slots.reshape(n_peers, slot_cap, model_width)
    returned = lax.all_to_all(back_slots, "expert", split_axis=0, concat_axis=0, tiled=True)
    route_parts = returned.reshape(n_slots, model_width)[slot_of_route]
    input_grad = jnp.sum(
        route_parts.reshape(tok_rows, top_k, model_width).astype(jnp.float32), axis=1
    ).astype(jnp.bfloat16)
    share_gate_up = lax.psum_scatter(
        sum_gate_up.astype(jnp.bfloat16), "dp", scatter_dimension=0, tiled=True
    ).astype(jnp.float32)
    share_down = lax.psum_scatter(
        sum_down.astype(jnp.bfloat16), "dp", scatter_dimension=0, tiled=True
    ).astype(jnp.float32)
    grad_gate = (grad_scale * share_gate_up[:, :hidden_width]).astype(jnp.bfloat16)[None]
    grad_up = (grad_scale * share_gate_up[:, hidden_width:]).astype(jnp.bfloat16)[None]
    grad_down = (grad_scale * share_down).astype(jnp.bfloat16)[None]
    return (input_grad, grad_gate, grad_up, grad_down)


def solution(mesh):
    return jax.shard_map(
        local,
        mesh=mesh,
        in_specs=(
            P(("dp", "expert"), None),
            P(("dp", "expert"), None),
            P(("dp", "expert"), None, None),
            P(("dp", "expert"), None),
            P(("dp", "expert"), None),
            P("expert", None, None),
            P("expert", None, None),
            P("expert", None, None),
        ),
        out_specs=(
            P(("dp", "expert"), None),
            P("expert", "dp", None),
            P("expert", "dp", None),
            P("expert", "dp", None),
        ),
        check_vma=False,
    )
```

profile of v0, /device:TPU:1, one launch (start us, length us, event | category | flops | bytes accessed | tf_op | source)
XLA Modules:
  0.0 729.3 jit_solution(16584094943626985307)
XLA Ops:
  7.2 0.7 broadcast_multiply_fusion
  7.9 0.8 copy.14
  9.3 1.7 reduce-window.15
  11.5 3.4 scatter_custom_fusion
  15.0 4.4 copy.18
  19.4 3.6 reshape.203
  23.1 6.1 gather_fusion.3
  29.2 3.9 broadcast_select_fusion.2
  33.1 8.8 %all-to-all-start.2 = ((bf16[32,48,1408]{2,1,0:T(8,128)(2,1)}), bf16[32,48,1408]{2,1,0:T(8,128)(2,1)}, u32[]{:S(2)}, u32[]{:S(2)}) async-start(bf16[32,48,1408]{2,1,0:T(8,128)(2,1)} %broadcast_select_fusion.2), calls=%async_computation.2 | async-start | bytes 8650752 | tf_op jit(solution)/shard_map/all_to_all | solution.py:84
  42.1 5.9 gather_fusion
  48.1 7.1 gather_fusion.1
  55.2 7.2 fusion.24
  62.4 31.0 %all-to-all-done.2 = bf16[32,48,1408]{2,1,0:T(8,128)(2,1)} async-done(((bf16[32,48,1408]{2,1,0:T(8,128)(2,1)}), bf16[32,48,1408]{2,1,0:T(8,128)(2,1)}, u32[]{:S(2)}, u32[]{:S(2)}) %all-to-all-start.2) | async-done | bytes 4325408 | tf_op jit(solution)/shard_map/all_to_all | solution.py:84
  93.4 8.4 %all-to-all-start = ((bf16[32,48,2048]{2,1,0:T(8,128)(2,1)}), bf16[32,48,2048]{2,1,0:T(8,128)(2,1)}, u32[]{:S(2)}, u32[]{:S(2)}) async-start(bf16[32,48,2048]{2,1,0:T(8,128)(2,1)} %fusion.24), calls=%async_computation | async-start | bytes 12582912 | tf_op jit(solution)/shard_map/all_to_all | solution.py:83
  101.8 7.0 gather_fusion.2
  108.9 5.9 broadcast_select_fusion.1
  114.8 60.1 %all-to-all-done = bf16[32,48,2048]{2,1,0:T(8,128)(2,1)} async-done(((bf16[32,48,2048]{2,1,0:T(8,128)(2,1)}), bf16[32,48,2048]{2,1,0:T(8,128)(2,1)}, u32[]{:S(2)}, u32[]{:S(2)}) %all-to-all-start) | async-done | bytes 6291488 | tf_op jit(solution)/shard_map/all_to_all | solution.py:83
  174.9 9.8 %all-to-all-start.1 = ((bf16[32,48,2048]{2,1,0:T(8,128)(2,1)}), bf16[32,48,2048]{2,1,0:T(8,128)(2,1)}, u32[]{:S(2)}, u32[]{:S(2)}) async-start(bf16[32,48,2048]{2,1,0:T(8,128)(2,1)} %broadcast_select_fusion.1), calls=%async_computation.1 | async-start | bytes 12582912 | tf_op jit(solution)/shard_map/all_to_all | solution.py:82
  184.6 0.5 reduce-scatter.5.cloned.1.call-start
  185.2 4.4 compare_reduce_fusion
  189.6 0.6 convert_reduce_fusion
  191.1 0.3 reduce-window.19
  191.7 0.6 fusion.41
  192.3 11.2 %scatter_custom_fusion.3 = bf16[1536,1408]{1,0:T(8,128)(2,1)} fusion(s32[1536]{0:T(1024)S(1)} %get-tuple-element.68, bf16[1536,1408]{1,0:T(8,128)(2,1)} %bitcast.8, bf16[]{:T(256)} %constant.73.clone.1), kind=kCustom, calls=%fused_computation.57 | custom fusion | bytes 4325888 | tf_op jit(solution)/shard_map/scatter | solution.py:105
  203.5 54.2 %all-to-all-done.1 = bf16[32,48,2048]{2,1,0:T(8,128)(2,1)} async-done(((bf16[32,48,2048]{2,1,0:T(8,128)(2,1)}), bf16[32,48,2048]{2,1,0:T(8,128)(2,1)}, u32[]{:S(2)}, u32[]{:S(2)}) %all-to-all-start.1) | async-done | bytes 6291488 | tf_op jit(solution)/shard_map/all_to_all | solution.py:82
  257.7 14.1 %scatter_custom_fusion.2 = bf16[1536,2048]{1,0:T(8,128)(2,1)} fusion(s32[1536]{0:T(1024)S(1)} %get-tuple-element.68, bf16[1536,2048]{1,0:T(8,128)(2,1)} %bitcast.5, bf16[]{:T(256)} %constant.73.clone.1), kind=kCustom, calls=%fused_computation.48 | custom fusion | bytes 6291968 | tf_op jit(solution)/shard_map/scatter | solution.py:95
  271.8 14.0 %scatter_custom_fusion.1 = bf16[1536,2048]{1,0:T(8,128)(2,1)} fusion(s32[1536]{0:T(1024)S(1)} %get-tuple-element.68, bf16[1536,2048]{1,0:T(8,128)(2,1)} %bitcast.2, bf16[]{:T(256)} %constant.73.clone.1), kind=kCustom, calls=%fused_computation.50 | custom fusion | bytes 6291968 | tf_op jit(solution)/shard_map/scatter | solution.py:100
  285.9 3.4 broadcast.169
  289.2 5.7 broadcast_in_dim.89
  294.9 9.1 %broadcast_in_dim.88 = f32[2048,2816]{1,0:T(8,128)} broadcast(f32[]{:T(128)} %constant.72.clone.1), dimensions={} | broadcast | bytes 23068676 | tf_op jit(solution)/shard_map/broadcast_in_dim | solution.py:124
  304.0 117.9 %while.14 = (s32[]{:T(128)}, bf16[1536,2048]{1,0:T(8,128)(2,1)}, f32[2048,2816]{1,0:T(8,128)}, f32[1408,2048]{1,0:T(8,128)}, s32[]{:T(128)}, /*index=5*/bf16[153...) while((s32[]{:T(128)}, bf16[1536,2048]{1,0:T(8,128)(2,1)}, ...), condition=%wide.region_12.13_spmd, body=%wide.region_11.12_spmd.sunk | while | flops 10354917376 | bytes 175245616 | solution.py:127
  304.3 4.9 fusion.75
  309.2 3.8 multiply_convert_fusion.7
  313.1 1.8 fusion.76
  314.9 2.9 fusion.77
  317.8 10.9 %convolution_add_fusion.6 = f32[1408,2048]{1,0:T(8,128)} fusion(f32[1408,2048]{1,0:T(8,128)} %get-tuple-element.189, bf16[1536,2048]{1,0:T(8,128)(2,1)} %get-tuple-element.206, s32[]{:T(128)S(6)} %select_n.129, f32[256,1408]{1,0:T(8,128)S(1)} %fusion.75, bf16[1536,1408]{1,0:T(8,128)(2,1)} %get-tuple-element.210), kind=kOutput, calls=%fused_computation.11.clone.1 | convolution fusion | flops 1481801728 | bytes 26280960 | tf_op jit(solution)/shard_map/while/body/dot_general | solution.py:36
  328.7 14.9 %convolution_add_fusion.5 = f32[2048,2816]{1,0:T(8,128)} fusion(f32[2048,2816]{1,0:T(8,128)} %get-tuple-element.188, bf16[256,1408]{1,0:T(8,128)(2,1)S(1)} %get-tuple-element.170, bf16[256,1408]{1,0:T(8,128)(2,1)S(1)} %get-tuple-element.169, bf16[1536,2048]{1,0:T(8,128)(2,1)} %get-tuple-element.208, s32[]{:T(128)S(6)} %select_n.129), kind=kOutput, calls=%fused_computation.10.clone.1 | convolution fusion | flops 2961440768 | bytes 48627716 | tf_op jit(solution)/shard_map/while/body/dot_general | solution.py:33
  343.6 4.9 fusion.75
  348.5 3.8 multiply_convert_fusion.7
  352.4 1.8 fusion.76
  354.2 2.9 fusion.77
  357.1 10.9 %convolution_add_fusion.6 = f32[1408,2048]{1,0:T(8,128)} fusion(f32[1408,2048]{1,0:T(8,128)} %get-tuple-element.189, bf16[1536,2048]{1,0:T(8,128)(2,1)} %get-tuple-element.206, s32[]{:T(128)S(6)} %select_n.129, f32[256,1408]{1,0:T(8,128)S(1)} %fusion.75, bf16[1536,1408]{1,0:T(8,128)(2,1)} %get-tuple-element.210), kind=kOutput, calls=%fused_computation.11.clone.1 | convolution fusion | flops 1481801728 | bytes 26280960 | tf_op jit(solution)/shard_map/while/body/dot_general | solution.py:36
  368.0 14.8 %convolution_add_fusion.5 = f32[2048,2816]{1,0:T(8,128)} fusion(f32[2048,2816]{1,0:T(8,128)} %get-tuple-element.188, bf16[256,1408]{1,0:T(8,128)(2,1)S(1)} %get-tuple-element.170, bf16[256,1408]{1,0:T(8,128)(2,1)S(1)} %get-tuple-element.169, bf16[1536,2048]{1,0:T(8,128)(2,1)} %get-tuple-element.208, s32[]{:T(128)S(6)} %select_n.129), kind=kOutput, calls=%fused_computation.10.clone.1 | convolution fusion | flops 2961440768 | bytes 48627716 | tf_op jit(solution)/shard_map/while/body/dot_general | solution.py:33
  382.8 4.9 fusion.75
  387.8 3.8 multiply_convert_fusion.7
  391.6 1.8 fusion.76
  393.5 2.8 fusion.77
  396.3 10.9 %convolution_add_fusion.6 = f32[1408,2048]{1,0:T(8,128)} fusion(f32[1408,2048]{1,0:T(8,128)} %get-tuple-element.189, bf16[1536,2048]{1,0:T(8,128)(2,1)} %get-tuple-element.206, s32[]{:T(128)S(6)} %select_n.129, f32[256,1408]{1,0:T(8,128)S(1)} %fusion.75, bf16[1536,1408]{1,0:T(8,128)(2,1)} %get-tuple-element.210), kind=kOutput, calls=%fused_computation.11.clone.1 | convolution fusion | flops 1481801728 | bytes 26280960 | tf_op jit(solution)/shard_map/while/body/dot_general | solution.py:36
  407.3 14.7 %convolution_add_fusion.5 = f32[2048,2816]{1,0:T(8,128)} fusion(f32[2048,2816]{1,0:T(8,128)} %get-tuple-element.188, bf16[256,1408]{1,0:T(8,128)(2,1)S(1)} %get-tuple-element.170, bf16[256,1408]{1,0:T(8,128)(2,1)S(1)} %get-tuple-element.169, bf16[1536,2048]{1,0:T(8,128)(2,1)} %get-tuple-element.208, s32[]{:T(128)S(6)} %select_n.129), kind=kOutput, calls=%fused_computation.10.clone.1 | convolution fusion | flops 2961440768 | bytes 48627716 | tf_op jit(solution)/shard_map/while/body/dot_general | solution.py:33
  422.0 7.6 %convert_element_type.81 = bf16[1408,2048]{1,0:T(8,128)(2,1)} convert(f32[1408,2048]{1,0:T(8,128)} %get-tuple-element.66) | non-fusion elementwise | flops 2883584 | bytes 17301504 | tf_op jit(solution)/shard_map/convert_element_type | solution.py:141
  429.6 0.3 reduce-scatter.3.cloned.1.call-start
  429.9 12.2 %convert_element_type.77 = bf16[2048,2816]{1,0:T(8,128)(2,1)} convert(f32[2048,2816]{1,0:T(8,128)} %get-tuple-element.65) | non-fusion elementwise | flops 5767168 | bytes 34603008 | tf_op jit(solution)/shard_map/convert_element_type | solution.py:138
  442.1 0.7 copy-done.5
  442.8 16.3 %gather_fusion.4 = bf16[1536,2048]{1,0:T(8,128)(2,1)} fusion(bf16[1536,2048]{1,0:T(8,128)(2,1)} %get-tuple-element.64, s32[2048]{0:T(1024)S(1)} %pad_clamp_fusion), kind=kCustom, calls=%fused_computation.4 | custom fusion | bytes 12589056 | tf_op jit(solution)/shard_map/gather | solution.py:129
  459.1 5.9 broadcast_select_fusion
  465.1 126.7 %all-to-all-start.3 = ((bf16[32,48,2048]{2,1,0:T(8,128)(2,1)}), bf16[32,48,2048]{2,1,0:T(8,128)(2,1)}, u32[]{:S(2)}, u32[]{:S(2)}) async-start(bf16[32,48,2048]{2,1,0:T(8,128)(2,1)} %broadcast_select_fusion), calls=%async_computation.3 | async-start | bytes 12582912 | tf_op jit(solution)/shard_map/all_to_all | solution.py:132
  591.8 72.9 %all-to-all-done.3 = bf16[32,48,2048]{2,1,0:T(8,128)(2,1)} async-done(((bf16[32,48,2048]{2,1,0:T(8,128)(2,1)}), bf16[32,48,2048]{2,1,0:T(8,128)(2,1)}, u32[]{:S(2)}, u32[]{:S(2)}) %all-to-all-start.3) | async-done | bytes 6291488 | tf_op jit(solution)/shard_map/all_to_all | solution.py:132
  664.8 10.9 %gather_fusion.5 = bf16[768,2048]{1,0:T(8,128)(2,1)} fusion(bf16[1536,2048]{1,0:T(8,128)(2,1)} %bitcast.11, s32[1024]{0:T(1024)S(1)} %pad_clamp_fusion.3), kind=kCustom, calls=%fused_computation.5 | custom fusion | bytes 6294528 | tf_op jit(solution)/shard_map/gather | solution.py:133
  675.6 6.3 reshape.206
  681.9 5.8 reduce_sum.35
  687.7 2.8 fusion.33
  690.5 27.2 %reduce-scatter.3.cloned.1.call-done = bf16[512,2816]{1,0:T(8,128)(2,1)} async-done(((bf16[2048,2816]{1,0:T(8,128)(2,1)}), bf16[512,2816]{1,0:T(8,128)(2,1)}) %reduce-scatter.3.cloned.1.call-update) | async-done | bytes 2883600 | tf_op jit(solution)/shard_map/reduce_scatter | solution.py:137
  717.7 2.3 convert_element_type.78
  719.9 2.0 fusion.35
  (73 shorter events, 2.0 us)
Async XLA Ops:
  7.2 40.9 %copy-start = (bf16[128,2048]{1,0:T(8,128)(2,1)S(1)}, bf16[128,2048]{1,0:T(8,128)(2,1)}, u32[]{:S(2)}) copy-start(bf16[128,2048]{1,0:T(8,128)(2,1)} %param.11) | copy-start | bytes 1572868
  11.4 3.5 copy-start.6
  33.1 8.8 %copy-start.8 = (f32[128,6]{0,1:T(8,128)S(1)}, f32[128,6]{0,1:T(8,128)}, u32[]{:S(2)}) copy-start(f32[128,6]{0,1:T(8,128)} %param.13) | copy-start | bytes 9220
  33.1 60.3 %all-to-all-start.2 = ((bf16[32,48,1408]{2,1,0:T(8,128)(2,1)}), bf16[32,48,1408]{2,1,0:T(8,128)(2,1)}, u32[]{:S(2)}, u32[]{:S(2)}) async-start(bf16[32,48,1408]{2,1,0:T(8,128)(2,1)} %broadcast_select_fusion.2), calls=%async_computation.2 | async-start | bytes 8650752 | tf_op jit(solution)/shard_map/all_to_all | solution.py:84
  62.4 39.5 %copy-start.2 = (bf16[128,2048]{1,0:T(8,128)(2,1)S(1)}, bf16[128,2048]{1,0:T(8,128)(2,1)}, u32[]{:S(2)}) copy-start(bf16[128,2048]{1,0:T(8,128)(2,1)} %param.10) | copy-start | bytes 1572868
  93.4 81.5 %all-to-all-start = ((bf16[32,48,2048]{2,1,0:T(8,128)(2,1)}), bf16[32,48,2048]{2,1,0:T(8,128)(2,1)}, u32[]{:S(2)}, u32[]{:S(2)}) async-start(bf16[32,48,2048]{2,1,0:T(8,128)(2,1)} %fusion.24), calls=%async_computation | async-start | bytes 12582912 | tf_op jit(solution)/shard_map/all_to_all | solution.py:83
  174.9 82.8 %all-to-all-start.1 = ((bf16[32,48,2048]{2,1,0:T(8,128)(2,1)}), bf16[32,48,2048]{2,1,0:T(8,128)(2,1)}, u32[]{:S(2)}, u32[]{:S(2)}) async-start(bf16[32,48,2048]{2,1,0:T(8,128)(2,1)} %broadcast_select_fusion.1), calls=%async_computation.1 | async-start | bytes 12582912 | tf_op jit(solution)/shard_map/all_to_all | solution.py:82
  184.6 503.1 %reduce-scatter.5.cloned.1.call-start = ((), (), s32[]{:S(2)}) async-start(), calls=%async_computation.7 | async-start | bytes 7208960 | tf_op jit(solution)/shard_map/reduce_scatter | solution.py:140
  189.6 96.3 %copy-start.3 = (pred[32,48]{1,0:T(8,128)(4,1)}, pred[32,48]{1,0:T(8,128)(4,1)S(1)}, u32[]{:S(2)}) copy-start(pred[32,48]{1,0:T(8,128)(4,1)S(1)} %compare_reduce_fusion) | copy-start | bytes 4612
  304.3 4.9 copy-start.9
  304.3 10.6 %slice-start = ((s8[5767168]{0:T(1024)(128)(4,1)}), s8[4194304]{0:T(1024)(128)(4,1)S(1)}, s32[]{:S(2)}) async-start(s8[5767168]{0:T(1024)(128)(4,1)} %bitcast.73), calls=%async_computation.8 | async-start | bytes 8388608 | tf_op jit(solution)/shard_map/while
  309.2 3.9 copy-start.10
  309.2 5.7 slice-start.1
  343.6 4.9 copy-start.9
  343.6 10.6 %slice-start = ((s8[5767168]{0:T(1024)(128)(4,1)}), s8[4194304]{0:T(1024)(128)(4,1)S(1)}, s32[]{:S(2)}) async-start(s8[5767168]{0:T(1024)(128)(4,1)} %bitcast.73), calls=%async_computation.8 | async-start | bytes 8388608 | tf_op jit(solution)/shard_map/while
  348.5 3.9 copy-start.10
  348.5 5.7 slice-start.1
  382.8 4.9 copy-start.9
  382.8 10.6 %slice-start = ((s8[5767168]{0:T(1024)(128)(4,1)}), s8[4194304]{0:T(1024)(128)(4,1)S(1)}, s32[]{:S(2)}) async-start(s8[5767168]{0:T(1024)(128)(4,1)} %bitcast.73), calls=%async_computation.8 | async-start | bytes 8388608 | tf_op jit(solution)/shard_map/while
  387.8 3.9 copy-start.10
  387.8 5.7 slice-start.1
  429.6 288.1 %reduce-scatter.3.cloned.1.call-start = ((), (), s32[]{:S(2)}) async-start(), calls=%async_computation.6 | async-start | bytes 14417920 | tf_op jit(solution)/shard_map/reduce_scatter | solution.py:137
  442.1 0.7 copy-start.5
  442.8 16.3 %copy-start.4 = (pred[32,48]{1,0:T(8,128)(4,1)S(1)}, pred[32,48]{1,0:T(8,128)(4,1)}, u32[]{:S(2)}) copy-start(pred[32,48]{1,0:T(8,128)(4,1)} %copy-done.3) | copy-start | bytes 4612
  465.1 126.7 %copy-start.7 = (s32[768]{0:T(1024)S(1)}, s32[768]{0:T(1024)}, u32[]{:S(2)}) copy-start(s32[768]{0:T(1024)} %copy-done.6) | copy-start | bytes 9220
  465.1 199.7 %all-to-all-start.3 = ((bf16[32,48,2048]{2,1,0:T(8,128)(2,1)}), bf16[32,48,2048]{2,1,0:T(8,128)(2,1)}, u32[]{:S(2)}, u32[]{:S(2)}) async-start(bf16[32,48,2048]{2,1,0:T(8,128)(2,1)} %broadcast_select_fusion), calls=%async_computation.3 | async-start | bytes 12582912 | tf_op jit(solution)/shard_map/all_to_all | solution.py:132
  717.7 4.3 copy-start.1
Sparse Core Ops, SparseCore 0:
  429.7 179.6 reduce-scatter.4
  611.8 105.7 reduce-scatter.2
where the time goes:
time: 737 us; the launch traced here: 729 us
  waiting for transfers between devices  245 us (33%)
  starting transfers between devices  154 us (21%)
  local copies, waits for them, and re-layouts  132 us (18%)
  matrix products  117 us (16%)
  other arithmetic  64.5 us (9%)
  between operations  15.4 us (2%)
    all_to_all x1, starting transfers between devices, local(): lax.all_to_all(back_slots, 'expert', split_axis=0, concat_axis=0, tiled=T...  127 us
    all_to_all x1, waiting for transfers between devices, local(): lax.all_to_all(back_slots, 'expert', split_axis=0, concat_axis=0, tiled=T...  72.9 us
    all_to_all x1, waiting for transfers between devices, local(): lax.all_to_all(send_grad, 'expert', split_axis=0, concat_axis=0, tiled=True)  60.1 us
    all_to_all x1, waiting for transfers between devices, local(): lax.all_to_all(send_rows, 'expert', split_axis=0, concat_axis=0, tiled=True)  54.2 us
    dot_general x3, matrix products, weight_terms(): lax.dot_general(rows_in, both_grads, contract_rows, preferred_element_typ...  44.4 us
    dot_general x3, matrix products, weight_terms(): lax.dot_general(hidden_act, routed_rows, contract_rows, preferred_element...  32.8 us
    all_to_all x1, waiting for transfers between devices, local(): lax.all_to_all(send_gate, 'expert', split_axis=0, concat_axis=0, tiled=True)  31 us
    reduce_scatter x1, waiting for transfers between devices, local(): lax.psum_scatter(sum_gate_up.astype(jnp.bfloat16), 'dp', scatter_dimensio...  27.2 us
  transfers between devices with their start and end apart: 6, of which 5 were waited for; matrix products, arithmetic and copies ran while one was open for 15% of the time, Pallas kernels for 0%

commit v1 on v0

v1 whole, which is shorter than its diff:
```python
import jax
import jax.numpy as jnp
from jax import lax
from jax.sharding import PartitionSpec as P

grad_scale = 0.0625
slot_cap = 48
gate_cuts = (0, 384, 896, 1408)


def mm(a, b, ca, cb):
    return lax.dot_general(a, b, (((ca,), (cb,)), ((), ())), preferred_element_type=jnp.float32)


def slot_onehot(chosen):
    n_tok = chosen.shape[1]
    before = (
        lax.broadcasted_iota(jnp.int32, (n_tok, n_tok), 0)
        < lax.broadcasted_iota(jnp.int32, (n_tok, n_tok), 1)
    ).astype(jnp.bfloat16)
    rank = mm(chosen.astype(jnp.bfloat16), before, 1, 0).astype(jnp.int32)
    slots = lax.broadcasted_iota(jnp.int32, (1, slot_cap, 1), 1)
    return (rank[:, None, :] == slots) & chosen[:, None, :]


def local(tokens, out_grad, gate_saved, probs, expert_ids, w_gate, w_up, w_down):
    n_peers = lax.axis_size("expert")
    me = lax.axis_index("expert")
    tok_rows, model_width = tokens.shape
    top_k = expert_ids.shape[1]
    hidden_width = w_up.shape[2]
    n_slots = n_peers * slot_cap
    gate_mat, up_mat, down_mat = w_gate[0], w_up[0], w_down[0]

    meta = jnp.concatenate([expert_ids.T.astype(jnp.float32), probs.T], axis=0)
    meta_all = lax.all_gather(meta, "expert", axis=0, tiled=False)
    rows_all = lax.all_gather(tokens, "expert", axis=0, tiled=True)
    grad_all = lax.all_gather(out_grad, "expert", axis=0, tiled=True)

    ids_t = expert_ids.T
    experts = lax.broadcasted_iota(jnp.int32, (n_peers, 1, 1), 0)
    named = ids_t[None] == experts
    send_hot = slot_onehot(jnp.any(named, axis=1))
    toks = lax.broadcasted_iota(jnp.int32, (1, top_k, tok_rows), 2)
    ks = lax.broadcasted_iota(jnp.int32, (1, top_k, tok_rows), 1)
    route_of = jnp.sum(jnp.where(named, toks * top_k + ks, 0), axis=1)
    route_of_slot = jnp.sum(jnp.where(send_hot, route_of[:, None, :], 0), axis=2)
    gate_rows = gate_saved.reshape(tok_rows * top_k, hidden_width)[route_of_slot.reshape(n_slots)]
    gate_rows = gate_rows.reshape(n_peers, slot_cap, hidden_width)
    recv_gate = [
        lax.all_to_all(
            gate_rows[:, :, a:b], "expert", split_axis=0, concat_axis=0, tiled=True
        ).reshape(n_slots, b - a)
        for a, b in zip(gate_cuts, gate_cuts[1:])
    ]

    mine = meta_all[:, :top_k, :] == me.astype(jnp.float32)
    prob_of = jnp.sum(jnp.where(mine, meta_all[:, top_k:, :], 0.0), axis=1)
    recv_hot = slot_onehot(jnp.any(mine, axis=1))
    tok_ids = lax.broadcasted_iota(jnp.int32, (1, 1, tok_rows), 2)
    src = lax.broadcasted_iota(jnp.int32, (n_peers, slot_cap), 0)
    row_of_slot = (src * tok_rows + jnp.sum(jnp.where(recv_hot, tok_ids, 0), axis=2)).reshape(n_slots)
    prob_of_slot = jnp.sum(jnp.where(recv_hot, prob_of[:, None, :], 0.0), axis=2).reshape(n_slots)
    used = jnp.any(recv_hot, axis=2).reshape(n_slots)
    rows_in = jnp.where(used[:, None], rows_all[row_of_slot], 0)
    routed = (prob_of_slot[:, None] * grad_all[row_of_slot].astype(jnp.float32)).astype(jnp.bfloat16)

    shares = []
    hidden, part = [], None
    for j, (a, b) in enumerate(zip(gate_cuts, gate_cuts[1:])):
        up_act = mm(rows_in, up_mat[:, a:b], 1, 0)
        hidden_grad = mm(routed, down_mat[a:b, :], 1, 1)
        gate_val = recv_gate[j].astype(jnp.float32)
        gate_sig = jax.nn.sigmoid(gate_val)
        gate_act = gate_val * gate_sig
        hidden.append((gate_act * up_act).astype(jnp.bfloat16))
        up_grad = (hidden_grad * gate_act).astype(jnp.bfloat16)
        gate_grad = (hidden_grad * up_act * gate_sig * (1.0 + gate_val * (1.0 - gate_sig))).astype(
            jnp.bfloat16
        )
        both = jnp.concatenate([gate_grad, up_grad], axis=1)
        term = mm(rows_in, both, 0, 0).astype(jnp.bfloat16)
        shares.append(lax.psum_scatter(term, "dp", scatter_dimension=0, tiled=True))
        piece = mm(gate_grad, gate_mat[:, a:b], 1, 1) + mm(up_grad, up_mat[:, a:b], 1, 1)
        part = piece if part is None else part + piece
    hidden_act = jnp.concatenate(hidden, axis=1)
    term_down = mm(hidden_act, routed, 0, 0).astype(jnp.bfloat16)
    share_down = lax.psum_scatter(term_down, "dp", scatter_dimension=0, tiled=True)

    back = part.astype(jnp.bfloat16).reshape(n_peers, slot_cap, model_width)
    returned = lax.all_to_all(back, "expert", split_axis=0, concat_axis=0, tiled=True)
    input_grad = mm(
        send_hot.reshape(n_slots, tok_rows).astype(jnp.bfloat16),
        returned.reshape(n_slots, model_width),
        0,
        0,
    ).astype(jnp.bfloat16)

    def scaled(share):
        return (grad_scale * share.astype(jnp.float32)).astype(jnp.bfloat16)

    widths = [b - a for a, b in zip(gate_cuts, gate_cuts[1:])]
    grad_gate = jnp.concatenate([scaled(s[:, :w]) for s, w in zip(shares, widths)], axis=1)[None]
    grad_up = jnp.concatenate([scaled(s[:, w:]) for s, w in zip(shares, widths)], axis=1)[None]
    return (input_grad, grad_gate, grad_up, scaled(share_down)[None])


def solution(mesh):
    return jax.shard_map(
        local,
        mesh=mesh,
        in_specs=(
            P(("dp", "expert"), None),
            P(("dp", "expert"), None),
            P(("dp", "expert"), None, None),
            P(("dp", "expert"), None),
            P(("dp", "expert"), None),
            P("expert", None, None),
            P("expert", None, None),
            P("expert", None, None),
        ),
        out_specs=(
            P(("dp", "expert"), None),
            P("expert", "dp", None),
            P("expert", "dp", None),
            P("expert", "dp", None),
        ),
        check_vma=False,
    )
```

time: 737 us -> 485 us (0.66)
  waiting for transfers between devices: 245 us -> 51.7 us
  blocking collectives: 0 us -> 144 us
  starting transfers between devices: 154 us -> 14.3 us
  local copies, waits for them, and re-layouts: 132 us -> 79.4 us
  other arithmetic: 64.5 us -> 15.2 us
  matrix products: 117 us -> 160 us
    all_to_all x4 -> x2, waiting for transfers between devices: 218 us -> 0.01 us  [local(): lax.all_to_all(gate_rows[:, :, a:b], 'expert', split_axis=0, concat_axis=...]
    all_to_all x4 -> x2, starting transfers between devices: 154 us -> 13.8 us  [local(): lax.all_to_all(gate_rows[:, :, a:b], 'expert', split_axis=0, concat_axis=...]
    all_to_all x0 -> x2, blocking collectives: none -> 106 us  [the longest x1 77.9 us: local(): lax.all_to_all(back, 'expert', split_axis=0, concat_axis=0, tiled=True)]
    all_gather x0 -> x2, waiting for transfers between devices: none -> 50.2 us  [the longest x1 49 us: local(): rows_all = lax.all_gather(tokens, 'expert', axis=0, tiled=True)]
    scatter x4 -> x0, local copies, waits for them, and re-layouts: 42.8 us -> none  [the longest x1 14.1 us: local(): dense_rows = jnp.zeros((padded_rows, model_width), jnp.bfloat16).at[dense...]
    dot_general x18 -> x19, matrix products: 117 us -> 160 us  [mm(): lax.dot_general(a, b, (((ca,), (cb,)), ((), ())), preferred_element_type=...]
    all_gather x0 -> x1, blocking collectives: none -> 37.6 us  [local(): meta_all = lax.all_gather(meta, 'expert', axis=0, tiled=False)]
    reduce_scatter x2 -> x4, waiting for transfers between devices: 27.2 us -> 0.05 us  [the longest x3 0.04 us: local(): shares.append(lax.psum_scatter(term, 'dp', scatter_dimension=0, tiled=True))]
  transfers between devices with their start and end apart: 6 -> 8, of which waited for: 5 -> 2; matrix products, arithmetic and copies ran while one was open for 15% -> 51% of each run, Pallas kernels for 0% -> 0%
where the time goes in v1:
time: 485 us; the launch traced here: 479 us
  matrix products  160 us (33%)
  blocking collectives  144 us (30%)
  local copies, waits for them, and re-layouts  79.4 us (16%)
  waiting for transfers between devices  51.7 us (11%)
  other arithmetic  15.2 us (3%)
  between operations  14.6 us (3%)
  starting transfers between devices  14.3 us (3%)
    dot_general x19, matrix products, mm(): lax.dot_general(a, b, (((ca,), (cb,)), ((), ())), preferred_element_type=...  160 us
    all_to_all x1, blocking collectives, local(): lax.all_to_all(back, 'expert', split_axis=0, concat_axis=0, tiled=True)  77.9 us
    all_gather x1, waiting for transfers between devices, local(): rows_all = lax.all_gather(tokens, 'expert', axis=0, tiled=True)  49 us
    all_gather x1, blocking collectives, local(): meta_all = lax.all_gather(meta, 'expert', axis=0, tiled=False)  37.6 us
    all_to_all x1, blocking collectives, local(): lax.all_to_all(gate_rows[:, :, a:b], 'expert', split_axis=0, concat_axis=...  28.2 us
    gather x1, local copies, waits for them, and re-layouts, local(): grad_all[row_of_slot].astype(jnp.float32)  20.6 us
    gather x1, local copies, waits for them, and re-layouts, local(): rows_in = jnp.where(used[:, None], rows_all[row_of_slot], 0)  20.6 us
    unnamed x67, local copies, waits for them, and re-layouts  13.8 us
  transfers between devices with their start and end apart: 8, of which 2 were waited for; matrix products, arithmetic and copies ran while one was open for 51% of the time, Pallas kernels for 0%

profile of v1, /device:TPU:1, one launch (start us, length us, event | category | flops | bytes accessed | tf_op | source)
XLA Modules:
  0.0 478.7 jit_solution(1710951057539450567)
XLA Ops:
  7.2 0.7 all-gather.5.cloned.1.call-update
  7.9 0.7 all-gather.7.cloned.1.call-update
  8.7 0.7 fusion.52
  9.4 0.7 select_reduce_fusion.3
  10.1 0.1 convolution_convert_fusion.5
  10.2 0.6 copy-done.9
  10.8 0.6 select_reduce_fusion
  11.6 4.4 copy.36
  16.0 3.6 reshape.119
  19.6 6.2 %gather_fusion.2 = bf16[1536,1408]{1,0:T(8,128)(2,1)} fusion(bf16[768,1408]{1,0:T(8,128)(2,1)S(1)} %reshape.119, s32[2048]{0:T(1024)S(1)} %pad_clamp_fusion), kind=kCustom, calls=%fused_computation.2 | custom fusion | bytes 8656896 | tf_op jit(solution)/shard_map/gather | solution.py:48
  25.8 2.4 slice.104
  28.2 8.6 %all-to-all-start = ((bf16[32,48,384]{2,1,0:T(8,128)(2,1)}), bf16[32,48,384]{2,1,0:T(8,128)(2,1)S(1)}, u32[]{:S(2)}, u32[]{:S(2)}) async-start(bf16[32,48,384]{2,1,0:T(8,128)(2,1)} %slice.104), calls=%async_computation | async-start | bytes 2359296 | tf_op jit(solution)/shard_map/all_to_all | solution.py:51
  36.9 37.6 %all-gather.1 = f32[32,12,128]{2,1,0:T(8,128)S(1)} all-gather(f32[1,12,128]{2,1,0:T(8,128)S(1)} %maximum_bitcast_fusion.2), channel_id=2, replica_groups=mesh['dp'=4,'expert'=32] {'expert'}, dimensions={0}, use_global_device_ids=true | all-gather | bytes 202752 | tf_op jit(solution)/shard_map/all_gather | solution.py:36
  74.6 0.1 convolution_convert_fusion.4
  74.7 0.3 select_reduce_fusion.2
  75.1 0.6 fusion.48
  75.7 0.7 broadcast_in_dim.88
  76.4 0.6 select_reduce_fusion.1
  77.3 4.2 fusion.59
  81.4 5.2 %all-to-all-start.1 = ((bf16[32,48,512]{2,1,0:T(8,128)(2,1)}), bf16[32,48,512]{2,1,0:T(8,128)(2,1)}, u32[]{:S(2)}, u32[]{:S(2)}) async-start(bf16[32,48,512]{2,1,0:T(8,128)(2,1)} %get-tuple-element.15), calls=%async_computation.1 | async-start | bytes 3145728 | tf_op jit(solution)/shard_map/all_to_all | solution.py:51
  86.6 0.3 reduce-scatter.5.cloned.1.call-start
  87.0 0.3 bitcast_convert_fusion.2
  87.2 2.0 copy.37
  89.2 1.2 all-gather.5.cloned.1.call-done
  90.4 20.6 %gather_fusion = bf16[1536,2048]{1,0:T(8,128)(2,1)} fusion(bf16[4096,2048]{1,0:T(8,128)(2,1)} %all-gather.5.cloned.1.call-done, s32[2048]{0:T(1024)S(1)} %pad_clamp_fusion.1), kind=kCustom, calls=%fused_computation | custom fusion | bytes 12589056 | tf_op jit(solution)/shard_map/gather | solution.py:66
  111.1 7.5 %fusion.38 = f32[1536,384]{0,1:T(8,128)} fusion(bf16[1,1408,2048]{2,1,0:T(8,128)(2,1)} %param.15, bf16[1536,2048]{1,0:T(8,128)(2,1)} %gather_fusion, f32[1536]{0:T(1024)S(1)} %mul.111), kind=kOutput, calls=%fused_computation.64 | convolution fusion | flops 2425356288 | bytes 10229760 | tf_op jit(solution)/shard_map/dot_general | solution.py:12
  118.6 49.0 %all-gather.7.cloned.1.call-done = bf16[4096,2048]{1,0:T(8,128)(2,1)} async-done(((bf16[128,2048]{1,0:T(8,128)(2,1)}), bf16[4096,2048]{1,0:T(8,128)(2,1)}) %all-gather.7.cloned.1.call-update) | async-done | bytes 16777232 | tf_op jit(solution)/shard_map/all_gather | solution.py:37
  167.5 20.6 %gather_fusion.1 = bf16[1536,2048]{1,0:T(8,128)(2,1)} fusion(bf16[4096,2048]{1,0:T(8,128)(2,1)} %all-gather.7.cloned.1.call-done, s32[2048]{0:T(1024)S(1)} %pad_clamp_fusion.1), kind=kCustom, calls=%fused_computation.1 | custom fusion | bytes 12589056 | tf_op jit(solution)/shard_map/gather | solution.py:65
  188.2 8.7 %multiply_convert_fusion.8 = (bf16[1536,384]{0,1:T(8,128)(2,1)}, bf16[1536,384]{0,1:T(8,128)(2,1)S(1)}, bf16[1536,384]{0,1:T(8,128)(2,1)S(1)}) fusion(f32[1536,384]{0,1:T(8,128)S(1)} %copy-done.4, f32[1536,384]{0,1:T(8,128)} %fusion.38, bf16[2048,1408]{1,0:T(8,128)(2,1)} %bitcast.58, bf16[1536,2048]{1,0:T(8,128)(2,1)} %gather_fusion.1, ...), kind=kOutput, calls=%fused_computation.37 | convolution fusion | flops 2427912192 | bytes 16123392 | tf_op jit(solution)/shard_map/dot_general | solution.py:12
  196.9 1.0 copy-done.5
  197.9 0.4 copy-done.7
  198.2 7.3 %convolution_convert_fusion.3 = bf16[2048,768]{1,0:T(8,128)(2,1)} fusion(bf16[1536,384]{0,1:T(8,128)(2,1)S(1)} %get-tuple-element.14, bf16[1536,384]{0,1:T(8,128)(2,1)S(1)} %get-tuple-element.13, bf16[1536,2048]{1,0:T(8,128)(2,1)S(1)} %copy-done.1, pred[1536]{0:T(1024)(128)(4,1)S(1)} %copy-done.15), kind=kOutput, calls=%fused_computation.14 | convolution fusion | flops 4841275392 | bytes 11798016 | tf_op jit(solution)/shard_map/dot_general | solution.py:12
  205.7 1.8 bitcast_convert_fusion.1
  207.5 2.6 copy.40
  210.1 6.6 %fusion.24 = f32[1536,512]{0,1:T(8,128)S(1)} fusion(bf16[1,1408,2048]{2,1,0:T(8,128)(2,1)} %param.15, bf16[1536,2048]{1,0:T(8,128)(2,1)} %gather_fusion, f32[1536]{0:T(1024)S(1)} %mul.111), kind=kOutput, calls=%fused_computation.48 | convolution fusion | flops 3230662656 | bytes 11540480 | tf_op jit(solution)/shard_map/dot_general | solution.py:12
  216.8 9.2 %multiply_convert_fusion.2 = (bf16[1536,512]{0,1:T(8,128)(2,1)}, bf16[1536,512]{0,1:T(8,128)(2,1)S(1)}, bf16[1536,512]{0,1:T(8,128)(2,1)S(1)}) fusion(f32[1536,512]{0,1:T(8,128)S(1)} %copy-done.2, f32[1536,512]{0,1:T(8,128)S(1)} %fusion.24, bf16[2048,1408]{1,0:T(8,128)(2,1)} %bitcast.59, bf16[1536,2048]{1,0:T(8,128)(2,1)} %gather_fusion.1, ...), kind=kOutput, calls=%fused_computation.22 | convolution fusion | flops 3236167680 | bytes 19400192 | tf_op jit(solution)/shard_map/dot_general | solution.py:12
  226.0 1.2 copy-done.16
  227.2 0.5 copy-done.18
  227.7 11.0 %convolution_convert_fusion.2 = bf16[2048,1024]{1,0:T(8,128)(2,1)} fusion(bf16[1536,512]{0,1:T(8,128)(2,1)S(1)} %get-tuple-element.8, bf16[1536,512]{0,1:T(8,128)(2,1)S(1)} %get-tuple-element.7, bf16[1536,2048]{1,0:T(8,128)(2,1)S(1)} %bitcast.52, pred[1536]{0:T(1024)(128)(4,1)S(1)} %copy-done.15), kind=kOutput, calls=%fused_computation.13 | convolution fusion | flops 6453985280 | bytes 13633024 | tf_op jit(solution)/shard_map/dot_general | solution.py:12
  238.8 1.4 copy-done
  240.2 28.2 %all_to_all.20 = bf16[32,48,512]{2,1,0:T(8,128)(2,1)S(1)} all-to-all(bf16[32,48,512]{2,1,0:T(8,128)(2,1)S(1)} %copy-done), channel_id=1, replica_groups=mesh['dp'=4,'expert'=32] {'expert'}, dimensions={0} | all-to-all | bytes 3145728 | tf_op jit(solution)/shard_map/all_to_all | solution.py:51
  268.4 0.5 bitcast_convert_fusion
  268.9 2.5 copy.43
  271.4 6.7 %fusion.22 = f32[1536,512]{0,1:T(8,128)S(1)} fusion(bf16[1,1408,2048]{2,1,0:T(8,128)(2,1)} %param.15, bf16[1536,2048]{1,0:T(8,128)(2,1)} %gather_fusion, f32[1536]{0:T(1024)S(1)} %mul.111), kind=kOutput, calls=%fused_computation.46 | convolution fusion | flops 3230662656 | bytes 11540480 | tf_op jit(solution)/shard_map/dot_general | solution.py:12
  278.1 9.2 %multiply_convert_fusion.1 = (bf16[1536,512]{0,1:T(8,128)(2,1)}, bf16[1536,512]{0,1:T(8,128)(2,1)S(1)}, bf16[1536,512]{0,1:T(8,128)(2,1)S(1)}) fusion(f32[1536,512]{0,1:T(8,128)S(1)} %copy-done.3, f32[1536,512]{0,1:T(8,128)S(1)} %fusion.22, bf16[2048,1408]{1,0:T(8,128)(2,1)} %bitcast.60, bf16[1536,2048]{1,0:T(8,128)(2,1)} %gather_fusion.1, ...), kind=kOutput, calls=%fused_computation.21 | convolution fusion | flops 3236167680 | bytes 19400192 | tf_op jit(solution)/shard_map/dot_general | solution.py:12
  287.4 1.2 copy-done.20
  288.5 0.5 copy-done.22
  289.0 11.0 %convolution_convert_fusion.1 = bf16[2048,1024]{1,0:T(8,128)(2,1)} fusion(bf16[1536,512]{0,1:T(8,128)(2,1)S(1)} %get-tuple-element.11, bf16[1536,512]{0,1:T(8,128)(2,1)S(1)} %get-tuple-element.10, bf16[1536,2048]{1,0:T(8,128)(2,1)S(1)} %bitcast.54, pred[1536]{0:T(1024)(128)(4,1)S(1)} %copy-done.15), kind=kOutput, calls=%fused_computation.12 | convolution fusion | flops 6453985280 | bytes 13633024 | tf_op jit(solution)/shard_map/dot_general | solution.py:12
  300.1 1.3 copy-done.19
  301.5 8.6 %fusion.32 = f32[1536,2048]{1,0:T(8,128)} fusion(bf16[1536,512]{0,1:T(8,128)(2,1)S(1)} %copy-done.19, bf16[2048,1408]{1,0:T(8,128)(2,1)} %bitcast.61), kind=kOutput, calls=%fused_computation.56 | convolution fusion | flops 3221225472 | bytes 16252928 | tf_op jit(solution)/shard_map/dot_general | solution.py:12
  310.1 8.2 %fusion.20 = f32[1536,2048]{1,0:T(8,128)} fusion(bf16[1536,512]{0,1:T(8,128)(2,1)S(1)} %copy-done.17, bf16[2048,1408]{1,0:T(8,128)(2,1)} %bitcast.55), kind=kOutput, calls=%fused_computation.44 | convolution fusion | flops 3221225472 | bytes 16252928 | tf_op jit(solution)/shard_map/dot_general | solution.py:12
  318.3 8.4 %fusion.18 = f32[1536,2048]{1,0:T(8,128)} fusion(bf16[1536,512]{0,1:T(8,128)(2,1)S(1)} %copy-done.23, bf16[2048,1408]{1,0:T(8,128)(2,1)} %bitcast.56), kind=kOutput, calls=%fused_computation.42 | convolution fusion | flops 3221225472 | bytes 16252928 | tf_op jit(solution)/shard_map/dot_general | solution.py:12
  326.7 13.9 %convolution_convert_fusion = bf16[1408,2048]{1,0:T(8,128)(2,1)} fusion(bf16[1536,512]{0,1:T(8,128)(2,1)S(1)} %copy-done.26, bf16[1536,512]{0,1:T(8,128)(2,1)S(1)} %copy-done.25, bf16[1536,384]{0,1:T(8,128)(2,1)S(1)} %copy-done.24, bf16[1536,2048]{1,0:T(8,128)(2,1)S(1)} %bitcast.50, f32[1536]{0:T(1024)S(1)} %mul.111), kind=kOutput, calls=%fused_computation.5 | convolution fusion | flops 8883666944 | bytes 16390144 | tf_op jit(solution)/shard_map/dot_general | solution.py:12
  340.6 1.2 copy-done.6
  341.9 7.8 %fusion.36 = f32[1536,2048]{1,0:T(8,128)} fusion(bf16[1536,384]{0,1:T(8,128)(2,1)S(1)} %copy-done.6, bf16[2048,1408]{1,0:T(8,128)(2,1)} %bitcast.57), kind=kOutput, calls=%fused_computation.60 | convolution fusion | flops 2415919104 | bytes 15335424 | tf_op jit(solution)/shard_map/dot_general | solution.py:12
  349.7 8.8 %fusion.28 = f32[1536,2048]{1,0:T(8,128)} fusion(bf16[1536,512]{0,1:T(8,128)(2,1)S(1)} %copy-done.21, bf16[2048,1408]{1,0:T(8,128)(2,1)} %bitcast.62), kind=kOutput, calls=%fused_computation.52 | convolution fusion | flops 3221225472 | bytes 16252928 | tf_op jit(solution)/shard_map/dot_general | solution.py:12
  358.5 24.7 %add_convert_fusion = bf16[1536,2048]{1,0:T(8,128)(2,1)} fusion(f32[1536,2048]{1,0:T(8,128)} %fusion.18, f32[1536,2048]{1,0:T(8,128)} %fusion.28, f32[1536,2048]{1,0:T(8,128)} %fusion.20, f32[1536,2048]{1,0:T(8,128)} %fusion.32, f32[1536,2048]{1,0:T(8,128)} %fusion.36, bf16[1536,384]{0,1:T(8,128)(2,1)S(1)} %copy-done.8, bf16[2048,1408]{1,0:T(8,128)(2,1)} %bitcast.63), kind=kOutput, calls=%fused_computation.3 | convolution fusion | flops 2434793472 | bytes 71958528 | tf_op jit(solution)/shard_map/dot_general | solution.py:12
  383.2 77.9 %all_to_all.21 = bf16[32,48,2048]{2,1,0:T(8,128)(2,1)S(1)} all-to-all(bf16[32,48,2048]{2,1,0:T(8,128)(2,1)} %bitcast.46), channel_id=1, replica_groups=mesh['dp'=4,'expert'=32] {'expert'}, dimensions={0} | all-to-all | bytes 12582912 | tf_op jit(solution)/shard_map/all_to_all | solution.py:91
  461.1 1.9 fusion.13
  462.9 1.3 multiply_convert_fusion.15
  464.2 1.4 multiply_convert_fusion.12
  465.6 1.4 multiply_convert_fusion.11
  467.0 1.8 maximum_bitcast_fusion
  468.9 2.8 fusion.41
  (89 shorter events, 1.0 us)
Async XLA Ops:
  7.2 83.3 %all-gather.5.cloned.1.call-start = ((), (), s32[]{:S(2)}) async-start(), calls=%async_computation.8 | async-start | bytes 17301504 | tf_op jit(solution)/shard_map/all_gather | solution.py:38
  7.9 159.6 %all-gather.7.cloned.1.call-start = ((), (), s32[]{:S(2)}) async-start(), calls=%async_computation.9 | async-start | bytes 17301504 | tf_op jit(solution)/shard_map/all_gather | solution.py:37
  9.4 0.9 copy-start.11
  10.2 0.6 copy-start.9
  25.8 11.0 %copy-start.13 = (s32[128,6]{0,1:T(8,128)S(1)}, s32[128,6]{0,1:T(8,128)}, u32[]{:S(2)}) copy-start(s32[128,6]{0,1:T(8,128)} %param.12) | copy-start | bytes 9220
  25.8 11.1 %copy-start.14 = (f32[128,6]{0,1:T(8,128)S(1)}, f32[128,6]{0,1:T(8,128)}, u32[]{:S(2)}) copy-start(f32[128,6]{0,1:T(8,128)} %param.11) | copy-start | bytes 9220
  28.2 53.2 %all-to-all-start = ((bf16[32,48,384]{2,1,0:T(8,128)(2,1)}), bf16[32,48,384]{2,1,0:T(8,128)(2,1)S(1)}, u32[]{:S(2)}, u32[]{:S(2)}) async-start(bf16[32,48,384]{2,1,0:T(8,128)(2,1)} %slice.104), calls=%async_computation | async-start | bytes 2359296 | tf_op jit(solution)/shard_map/all_to_all | solution.py:51
  81.4 124.2 %all-to-all-start.1 = ((bf16[32,48,512]{2,1,0:T(8,128)(2,1)}), bf16[32,48,512]{2,1,0:T(8,128)(2,1)}, u32[]{:S(2)}, u32[]{:S(2)}) async-start(bf16[32,48,512]{2,1,0:T(8,128)(2,1)} %get-tuple-element.15), calls=%async_computation.1 | async-start | bytes 3145728 | tf_op jit(solution)/shard_map/all_to_all | solution.py:51
  86.6 376.3 %reduce-scatter.5.cloned.1.call-start = ((), (), s32[]{:S(2)}) async-start(), calls=%async_computation.10 | async-start | bytes 3932160 | tf_op jit(solution)/shard_map/reduce_scatter | solution.py:83
  118.6 69.6 %copy-start.4 = (f32[1536,384]{0,1:T(8,128)S(1)}, f32[1536,384]{0,1:T(8,128)}, u32[]{:S(2)}) copy-start(f32[1536,384]{0,1:T(8,128)} %copy.37) | copy-start | bytes 7077892
  118.6 69.6 %copy-start.15 = (pred[1536]{0:T(1024)(128)(4,1)S(1)}, pred[1536]{0:T(1024)(128)(4,1)}, u32[]{:S(2)}) copy-start(pred[1536]{0:T(1024)(128)(4,1)} %broadcast_in_dim.88) | copy-start | bytes 4612
  188.2 10.1 %copy-start.1 = (bf16[1536,2048]{1,0:T(8,128)(2,1)S(1)}, bf16[1536,2048]{1,0:T(8,128)(2,1)}, u32[]{:S(2)}) copy-start(bf16[1536,2048]{1,0:T(8,128)(2,1)} %gather_fusion.1) | copy-start | bytes 18874372
  196.8 1.0 copy-start.5
  196.8 1.4 copy-start.7
  205.6 258.6 %reduce-scatter.7.cloned.1.call-start = ((), (), s32[]{:S(2)}) async-start(), calls=%async_computation.11 | async-start | bytes 5242880 | tf_op jit(solution)/shard_map/reduce_scatter | solution.py:83
  210.1 6.6 %copy-start.2 = (f32[1536,512]{0,1:T(8,128)S(1)}, f32[1536,512]{0,1:T(8,128)}, u32[]{:S(2)}) copy-start(f32[1536,512]{0,1:T(8,128)} %copy.40) | copy-start | bytes 9437188
  210.1 17.6 %slice-start.2 = ((s8[6291456]{0:T(1024)(128)(4,1)}), s8[4194304]{0:T(1024)(128)(4,1)S(1)}, s32[]{:S(2)}) async-start(s8[6291456]{0:T(1024)(128)(4,1)} %bitcast.51), calls=%async_computation.16 | async-start | bytes 8388608
  216.8 10.9 %slice-start.3 = ((s8[6291456]{0:T(1024)(128)(4,1)}), s8[2097152]{0:T(1024)(128)(4,1)S(1)}, s32[]{:S(2)}) async-start(s8[6291456]{0:T(1024)(128)(4,1)} %bitcast.51), calls=%async_computation.17 | async-start | bytes 4194304
  226.0 1.2 copy-start.16
  226.0 1.7 copy-start.18
  238.7 1.4 copy-start
  238.8 226.9 %reduce-scatter.9.cloned.1.call-start = ((), (), s32[]{:S(2)}) async-start(), calls=%async_computation.12 | async-start | bytes 5242880 | tf_op jit(solution)/shard_map/reduce_scatter | solution.py:83
  271.4 6.7 %copy-start.3 = (f32[1536,512]{0,1:T(8,128)S(1)}, f32[1536,512]{0,1:T(8,128)}, u32[]{:S(2)}) copy-start(f32[1536,512]{0,1:T(8,128)} %copy.43) | copy-start | bytes 9437188
  271.4 17.6 %slice-start.4 = ((s8[6291456]{0:T(1024)(128)(4,1)}), s8[4194304]{0:T(1024)(128)(4,1)S(1)}, s32[]{:S(2)}) async-start(s8[6291456]{0:T(1024)(128)(4,1)} %bitcast.53), calls=%async_computation.18 | async-start | bytes 8388608
  278.1 10.9 %slice-start.5 = ((s8[6291456]{0:T(1024)(128)(4,1)}), s8[2097152]{0:T(1024)(128)(4,1)S(1)}, s32[]{:S(2)}) async-start(s8[6291456]{0:T(1024)(128)(4,1)} %bitcast.53), calls=%async_computation.19 | async-start | bytes 4194304
  287.4 1.2 copy-start.20
  287.4 1.6 copy-start.22
  300.1 1.4 copy-start.19
  300.1 10.0 %copy-start.17 = (bf16[1536,512]{0,1:T(8,128)(2,1)S(1)}, bf16[1536,512]{0,1:T(8,128)(2,1)}, u32[]{:S(2)}) copy-start(bf16[1536,512]{0,1:T(8,128)(2,1)} %copy-done.16) | copy-start | bytes 4718596
  300.1 168.8 %reduce-scatter.11.cloned.1.call-start = ((), (), s32[]{:S(2)}) async-start(), calls=%async_computation.13 | async-start | bytes 7208960 | tf_op jit(solution)/shard_map/reduce_scatter | solution.py:88
  310.1 8.2 %copy-start.23 = (bf16[1536,512]{0,1:T(8,128)(2,1)S(1)}, bf16[1536,512]{0,1:T(8,128)(2,1)}, u32[]{:S(2)}) copy-start(bf16[1536,512]{0,1:T(8,128)(2,1)} %copy-done.22) | copy-start | bytes 4718596
  310.1 16.6 %slice-start = ((s8[6291456]{0:T(1024)(128)(4,1)}), s8[4194304]{0:T(1024)(128)(4,1)S(1)}, s32[]{:S(2)}) async-start(s8[6291456]{0:T(1024)(128)(4,1)} %bitcast.49), calls=%async_computation.14 | async-start | bytes 8388608
  318.3 8.4 %slice-start.1 = ((s8[6291456]{0:T(1024)(128)(4,1)}), s8[2097152]{0:T(1024)(128)(4,1)S(1)}, s32[]{:S(2)}) async-start(s8[6291456]{0:T(1024)(128)(4,1)} %bitcast.49), calls=%async_computation.15 | async-start | bytes 4194304
  318.3 8.4 %copy-start.24 = (bf16[1536,384]{0,1:T(8,128)(2,1)S(1)}, bf16[1536,384]{0,1:T(8,128)(2,1)}, u32[]{:S(2)}) copy-start(bf16[1536,384]{0,1:T(8,128)(2,1)} %get-tuple-element.12) | copy-start | bytes 3538948
  318.3 8.4 %copy-start.25 = (bf16[1536,512]{0,1:T(8,128)(2,1)S(1)}, bf16[1536,512]{0,1:T(8,128)(2,1)}, u32[]{:S(2)}) copy-start(bf16[1536,512]{0,1:T(8,128)(2,1)} %get-tuple-element.6) | copy-start | bytes 4718596
  318.3 8.4 %copy-start.26 = (bf16[1536,512]{0,1:T(8,128)(2,1)S(1)}, bf16[1536,512]{0,1:T(8,128)(2,1)}, u32[]{:S(2)}) copy-start(bf16[1536,512]{0,1:T(8,128)(2,1)} %get-tuple-element.9) | copy-start | bytes 4718596
  340.6 1.3 copy-start.6
  341.9 7.8 %copy-start.21 = (bf16[1536,512]{0,1:T(8,128)(2,1)S(1)}, bf16[1536,512]{0,1:T(8,128)(2,1)}, u32[]{:S(2)}) copy-start(bf16[1536,512]{0,1:T(8,128)(2,1)} %copy-done.20) | copy-start | bytes 4718596
  349.7 8.8 %copy-start.8 = (bf16[1536,384]{0,1:T(8,128)(2,1)S(1)}, bf16[1536,384]{0,1:T(8,128)(2,1)}, u32[]{:S(2)}) copy-start(bf16[1536,384]{0,1:T(8,128)(2,1)} %copy-done.7) | copy-start | bytes 3538948
  383.2 77.9 %copy-start.10 = (s32[32,128]{1,0:T(8,128)S(1)}, s32[32,128]{1,0:T(8,128)}, u32[]{:S(2)}) copy-start(s32[32,128]{1,0:T(8,128)} %copy-done.9) | copy-start | bytes 49156
  383.2 77.9 %copy-start.12 = (pred[32,128]{1,0:T(8,128)(4,1)S(1)}, pred[32,128]{1,0:T(8,128)(4,1)}, u32[]{:S(2)}) copy-start(pred[32,128]{1,0:T(8,128)(4,1)} %copy-done.11) | copy-start | bytes 12292
Sparse Core Ops, SparseCore 0:
  10.3 80.1 all-gather.4
  92.7 74.8 all-gather.6
  205.7 37.6 reduce-scatter.4
  245.7 46.6 reduce-scatter.6
  300.2 44.5 reduce-scatter.8
  347.1 59.4 reduce-scatter.10

commit v2 on v1

v2 whole, which is shorter than its diff:
```python
import functools

import jax
import jax.numpy as jnp
from jax import lax
from jax.experimental import pallas as pl
from jax.experimental.pallas import tpu as pltpu
from jax.sharding import PartitionSpec as P

grad_scale = 0.0625
slot_cap = 48
gate_cuts = (0, 640, 1408)


def mm(a, b, ca, cb):
    return lax.dot_general(a, b, (((ca,), (cb,)), ((), ())), preferred_element_type=jnp.float32)


def slot_of_token(chosen):
    n_tok = chosen.shape[1]
    before = (
        lax.broadcasted_iota(jnp.int32, (n_tok, n_tok), 0)
        < lax.broadcasted_iota(jnp.int32, (n_tok, n_tok), 1)
    ).astype(jnp.bfloat16)
    rank = mm(chosen.astype(jnp.bfloat16), before, 1, 0).astype(jnp.int32)
    return jnp.where(chosen, rank, -1)


def pick_kernel(with_prob, slot_ref, prob_ref, own_ref, other_ref, out_ref):
    rows, toks = out_ref.shape[0], own_ref.shape[0]
    hit = lax.broadcasted_iota(jnp.int32, (rows, 2 * toks), 0) == slot_ref[0]
    hot = hit.astype(jnp.float32).astype(jnp.bfloat16)
    got = jnp.dot(hot[:, :toks], own_ref[...], preferred_element_type=jnp.float32)
    got = got + jnp.dot(hot[:, toks:], other_ref[...], preferred_element_type=jnp.float32)
    if with_prob:
        got = got * jnp.sum(jnp.where(hit, prob_ref[0], 0.0), axis=1, keepdims=True)
    out_ref[...] = got.astype(out_ref.dtype)


def pick(slots, probs, own, other, with_prob):
    chips, _, pair = slots.shape
    tok, width = pair // 2, own.shape[1]
    rows = 2 * slot_cap
    small = pl.BlockSpec((1, 1, pair), lambda i: (i, 0, 0))
    big = pl.BlockSpec((tok, width), lambda i: (i, 0))
    return pl.pallas_call(
        functools.partial(pick_kernel, with_prob),
        out_shape=jax.ShapeDtypeStruct((chips * rows, width), jnp.bfloat16),
        grid=(chips,),
        in_specs=[small, small, big, big],
        out_specs=pl.BlockSpec((rows, width), lambda i: (i, 0)),
        compiler_params=pltpu.CompilerParams(vmem_limit_bytes=24 << 20),
        cost_estimate=pl.CostEstimate(
            flops=2 * chips * rows * pair * width, bytes_accessed=4 * chips * pair * width, transcendentals=0
        ),
    )(slots, probs, own, other)


def back_kernel(cuts, *refs):
    n = len(cuts) - 1
    gate_ref, up_ref, out_ref = refs[2 * n :]
    total = None
    for j, (a, b) in enumerate(zip(cuts, cuts[1:])):
        term = mm(refs[j][...], gate_ref[:, a:b], 1, 1) + mm(refs[n + j][...], up_ref[:, a:b], 1, 1)
        total = term if total is None else total + term
    out_ref[...] = total.astype(out_ref.dtype)


def input_parts(grads, gate_mat, up_mat):
    n_slots = grads[0].shape[0]
    width, hidden = gate_mat.shape
    tile = 256
    whole = pl.BlockSpec((width, hidden), lambda i: (0, 0), pipeline_mode=pl.Buffered(1))
    return pl.pallas_call(
        functools.partial(back_kernel, gate_cuts),
        out_shape=jax.ShapeDtypeStruct((n_slots, width), jnp.bfloat16),
        grid=(n_slots // tile,),
        in_specs=[pl.BlockSpec((tile, b.shape[1]), lambda i: (i, 0)) for b in grads] + [whole, whole],
        out_specs=pl.BlockSpec((tile, width), lambda i: (i, 0)),
        compiler_params=pltpu.CompilerParams(vmem_limit_bytes=40 << 20),
        cost_estimate=pl.CostEstimate(
            flops=4 * n_slots * hidden * width, bytes_accessed=4 * hidden * width, transcendentals=0
        ),
    )(*grads, gate_mat, up_mat)


def local(tokens, out_grad, gate_saved, probs, expert_ids, w_gate, w_up, w_down):
    n_peers = lax.axis_size("expert")
    me = lax.axis_index("expert")
    core = me % 2
    tok_rows, model_width = tokens.shape
    top_k = expert_ids.shape[1]
    hidden_width = w_up.shape[2]
    n_slots = n_peers * slot_cap
    n_chips = n_peers // 2
    gate_mat, up_mat, down_mat = w_gate[0], w_up[0], w_down[0]
    same_core = [[2 * i + c for i in range(n_chips)] for c in range(2)]
    swap = [(i, i ^ 1) for i in range(n_peers)]

    meta = jnp.concatenate([expert_ids.T.astype(jnp.float32), probs.T], axis=0)
    meta_all = lax.all_gather(meta, "expert", axis=0, tiled=False)
    grad_own = lax.all_gather(out_grad, "expert", axis=0, tiled=True, axis_index_groups=same_core)
    rows_own = lax.all_gather(tokens, "expert", axis=0, tiled=True, axis_index_groups=same_core)

    ids_t = expert_ids.T
    experts = lax.broadcasted_iota(jnp.int32, (n_peers, 1, 1), 0)
    named = ids_t[None] == experts
    send_slot = slot_of_token(jnp.any(named, axis=1))
    slots = lax.broadcasted_iota(jnp.int32, (1, slot_cap, 1), 1)
    send_hot = send_slot[:, None, :] == slots
    toks = lax.broadcasted_iota(jnp.int32, (1, top_k, tok_rows), 2)
    ks = lax.broadcasted_iota(jnp.int32, (1, top_k, tok_rows), 1)
    route_of = jnp.sum(jnp.where(named, toks * top_k + ks, 0), axis=1)
    route_of_slot = jnp.sum(jnp.where(send_hot, route_of[:, None, :], 0), axis=2)
    route_of_slot, meta_all = lax.optimization_barrier((route_of_slot, meta_all))
    gate_rows = gate_saved.reshape(tok_rows * top_k, hidden_width)[route_of_slot.reshape(n_slots)]
    gate_rows = gate_rows.reshape(n_peers, slot_cap, hidden_width)
    def own_first(x):
        x = x.reshape(n_chips, 2, tok_rows)
        return jnp.where(core == 0, x, x[:, ::-1]).reshape(n_chips, 1, 2 * tok_rows)

    recv_gate = []
    for j, (a, b) in enumerate(zip(gate_cuts, gate_cuts[1:])):
        cut = gate_rows[:, :, a:b]
        if j > 0:
            cut, _ = lax.optimization_barrier((cut, rows_own))
        got = lax.all_to_all(cut, "expert", split_axis=0, concat_axis=0, tiled=True)
        if j == 0:
            got, grad_own = lax.optimization_barrier((got, grad_own))
        recv_gate.append(got.reshape(n_slots, b - a))
    grad_other = lax.ppermute(grad_own, "expert", swap)
    rows_other = lax.ppermute(rows_own, "expert", swap)

    mine = meta_all[:, :top_k, :] == me.astype(jnp.float32)
    prob_of = own_first(jnp.sum(jnp.where(mine, meta_all[:, top_k:, :], 0.0), axis=1))
    recv_slot = slot_of_token(jnp.any(mine, axis=1))
    odd = lax.broadcasted_iota(jnp.int32, recv_slot.shape, 0) % 2
    recv_slot = own_first(jnp.where(recv_slot >= 0, recv_slot + slot_cap * odd, -1))
    routed = pick(recv_slot, prob_of, grad_own, grad_other, True)
    rows_in = pick(recv_slot, prob_of, rows_own, rows_other, False)

    shares, hidden, gate_grads, up_grads = [], [], [], []
    for j, (a, b) in enumerate(zip(gate_cuts, gate_cuts[1:])):
        hidden_grad = mm(routed, down_mat[a:b, :], 1, 1)
        up_act = mm(rows_in, up_mat[:, a:b], 1, 0)
        gate_val = recv_gate[j].astype(jnp.float32)
        gate_sig = jax.nn.sigmoid(gate_val)
        gate_act = gate_val * gate_sig
        hidden.append((gate_act * up_act).astype(jnp.bfloat16))
        up_grad = (hidden_grad * gate_act).astype(jnp.bfloat16)
        gate_grad = (hidden_grad * up_act * gate_sig * (1.0 + gate_val * (1.0 - gate_sig))).astype(
            jnp.bfloat16
        )
        both = jnp.concatenate([gate_grad, up_grad], axis=1)
        gate_grads.append(gate_grad)
        up_grads.append(up_grad)
        term = (grad_scale * mm(rows_in, both, 0, 0)).astype(jnp.bfloat16)
        shares.append(lax.psum_scatter(term, "dp", scatter_dimension=0, tiled=True))

    hidden_act = jnp.concatenate(hidden, axis=1)
    term_down = (grad_scale * mm(hidden_act, routed, 0, 0)).astype(jnp.bfloat16)
    grads, term_down = lax.optimization_barrier((gate_grads + up_grads, term_down))
    grad_down = lax.psum_scatter(term_down, "dp", scatter_dimension=0, tiled=True)

    back = input_parts(grads, gate_mat, up_mat).reshape(n_peers, slot_cap, model_width)
    returned = lax.all_to_all(back, "expert", split_axis=0, concat_axis=0, tiled=True)
    input_grad = mm(
        send_hot.reshape(n_slots, tok_rows).astype(jnp.bfloat16),
        returned.reshape(n_slots, model_width),
        0,
        0,
    ).astype(jnp.bfloat16)

    widths = [b - a for a, b in zip(gate_cuts, gate_cuts[1:])]
    grad_gate = jnp.concatenate([s[:, :w] for s, w in zip(shares, widths)], axis=1)
    grad_up = jnp.concatenate([s[:, w:] for s, w in zip(shares, widths)], axis=1)
    return (input_grad, grad_gate[None], grad_up[None], grad_down[None])


def solution(mesh):
    return jax.shard_map(
        local,
        mesh=mesh,
        in_specs=(
            P(("dp", "expert"), None),
            P(("dp", "expert"), None),
            P(("dp", "expert"), None, None),
            P(("dp", "expert"), None),
            P(("dp", "expert"), None),
            P("expert", None, None),
            P("expert", None, None),
            P("expert", None, None),
        ),
        out_specs=(
            P(("dp", "expert"), None),
            P("expert", "dp", None),
            P("expert", "dp", None),
            P("expert", "dp", None),
        ),
        check_vma=False,
    )
```

time: 485 us -> 453 us (0.934)
  matrix products: 160 us -> 82.4 us
  Pallas kernels: 0 us -> 49 us
  waiting for transfers between devices: 51.7 us -> 96.2 us
  local copies, waits for them, and re-layouts: 79.4 us -> 37.3 us
  blocking collectives: 144 us -> 158 us
  other arithmetic: 15.2 us -> 3.28 us
  starting transfers between devices: 14.3 us -> 7.01 us
    dot_general x19 -> x10, matrix products: 160 us -> 82.4 us  [mm(): lax.dot_general(a, b, (((ca,), (cb,)), ((), ())), preferred_element_type=...]
    pallas_call x0 -> x3, Pallas kernels: none -> 49 us  [the longest x2 24.7 us: pick(): pl.pallas_call(functools.partial(pick_kernel, with_prob), out_shape=jax.S...]
    gather x2 -> x0, local copies, waits for them, and re-layouts: 41.3 us -> none  [the longest x1 20.6 us: local(): grad_all[row_of_slot].astype(jnp.float32)]
    all_gather x2, waiting for transfers between devices: 50.2 us -> 73.8 us  [the longest x1 71.9 us: local(): lax.all_gather(tokens, 'expert', axis=0, tiled=True, axis_index_groups=sa...]
    all_to_all x1, blocking collectives: 28.2 us -> 51.2 us  [local(): got = lax.all_to_all(cut, 'expert', split_axis=0, concat_axis=0, tiled=True)]
    all_to_all x2 -> x1, waiting for transfers between devices: 0.01 us -> 21 us  [local(): got = lax.all_to_all(cut, 'expert', split_axis=0, concat_axis=0, tiled=True)]
    all_gather x1, blocking collectives: 37.6 us -> 26.5 us  [local(): meta_all = lax.all_gather(meta, 'expert', axis=0, tiled=False)]
    all_to_all x2 -> x1, starting transfers between devices: 13.8 us -> 5.46 us  [local(): got = lax.all_to_all(cut, 'expert', split_axis=0, concat_axis=0, tiled=True)]
  transfers between devices with their start and end apart: 8 -> 8, of which waited for: 2 -> 3; matrix products, arithmetic and copies ran while one was open for 51% -> 19% of each run, Pallas kernels for 0% -> 8%
where the time goes in v2:
time: 453 us; the launch traced here: 447 us
  blocking collectives  158 us (35%)
  waiting for transfers between devices  96.2 us (21%)
  matrix products  82.4 us (18%)
  Pallas kernels  49 us (11%)
  local copies, waits for them, and re-layouts  37.3 us (8%)
  between operations  14.3 us (3%)
  starting transfers between devices  7.01 us (2%)
    dot_general x10, matrix products, mm(): lax.dot_general(a, b, (((ca,), (cb,)), ((), ())), preferred_element_type=...  82.4 us
    all_to_all x1, blocking collectives, local(): lax.all_to_all(back, 'expert', split_axis=0, concat_axis=0, tiled=True)  80.1 us
    all_gather x1, waiting for transfers between devices, local(): lax.all_gather(tokens, 'expert', axis=0, tiled=True, axis_index_groups=sa...  71.9 us
    all_to_all x1, blocking collectives, local(): got = lax.all_to_all(cut, 'expert', split_axis=0, concat_axis=0, tiled=True)  51.2 us
    all_gather x1, blocking collectives, local(): meta_all = lax.all_gather(meta, 'expert', axis=0, tiled=False)  26.5 us
    pallas_call x2, Pallas kernels, pick(): pl.pallas_call(functools.partial(pick_kernel, with_prob), out_shape=jax.S...  24.7 us
    pallas_call x1, Pallas kernels, input_parts(): pl.pallas_call(functools.partial(back_kernel, gate_cuts), out_shape=jax.S...  24.3 us
    all_to_all x1, waiting for transfers between devices, local(): got = lax.all_to_all(cut, 'expert', split_axis=0, concat_axis=0, tiled=True)  21 us
  transfers between devices with their start and end apart: 8, of which 3 were waited for; matrix products, arithmetic and copies ran while one was open for 19% of the time, Pallas kernels for 8%

profile of v2, /device:TPU:1, one launch (start us, length us, event | category | flops | bytes accessed | tf_op | source)
XLA Modules:
  0.0 447.3 jit_solution(8524580425765071854)
XLA Ops:
  7.2 0.0 all-gather.5.cloned.1.call-start
  7.2 0.7 all-gather.5.cloned.1.call-update
  7.9 0.0 all-gather.7.cloned.1.call-start
  7.9 0.7 all-gather.7.cloned.1.call-update
  8.6 0.0 copy-start.11
  8.7 0.0 copy-start.12
  8.7 0.0 reduce-scatter.4.cloned.1.call-start
  8.7 4.4 copy.39
  13.1 3.6 reshape.95
  16.8 0.0 copy-done.11
  16.8 0.0 copy-done.12
  16.8 26.5 %all-gather.1 = f32[32,12,128]{2,1,0:T(8,128)S(1)} all-gather(f32[1,12,128]{2,1,0:T(8,128)S(1)} %maximum_bitcast_fusion.2), channel_id=2, replica_groups=mesh['dp'=4,'expert'=32] {'expert'}, dimensions={0}, use_global_device_ids=true | all-gather | bytes 202752 | tf_op jit(solution)/shard_map/all_gather | solution.py:101
  43.3 0.1 fusion.33
  43.5 0.6 select_reduce_fusion
  44.1 0.1 reshape.96
  44.2 6.1 %gather_fusion = bf16[1536,1408]{1,0:T(8,128)(2,1)} fusion(bf16[768,1408]{1,0:T(8,128)(2,1)S(1)} %reshape.95, s32[2048]{0:T(1024)S(1)} %pad_clamp_fusion), kind=kCustom, calls=%fused_computation | custom fusion | bytes 8656896 | tf_op jit(solution)/shard_map/gather | solution.py:116
  50.4 1.7 slice.58
  52.1 51.2 %all_to_all.15 = bf16[32,48,640]{2,1,0:T(8,128)(2,1)} all-to-all(bf16[32,48,640]{2,1,0:T(8,128)(2,1)S(1)} %slice.58), channel_id=1, replica_groups=mesh['dp'=4,'expert'=32] {'expert'}, dimensions={0} | all-to-all | bytes 3932160 | tf_op jit(solution)/shard_map/all_to_all | solution.py:127
  103.3 1.9 all-gather.5.cloned.1.call-done.own_ref
  105.2 0.7 collective-permute-start
  105.9 71.9 %all-gather.7.cloned.1.call-done.own_ref = bf16[2048,2048]{1,0:T(8,128)(2,1)} async-done(((bf16[128,2048]{1,0:T(8,128)(2,1)}), bf16[2048,2048]{1,0:T(8,128)(2,1)}) %all-gather.7.cloned.1.call-update) | async-done | bytes 8388624 | tf_op jit(solution)/shard_map/all_gather | solution.py:103
  177.8 0.7 collective-permute-start.1
  178.4 0.1 select_reduce_fusion.1
  178.5 0.1 reduce_or.19
  178.6 0.1 add_select_fusion
  178.9 0.0 collective-permute-done.other_ref
  178.9 0.0 copy-start
  178.9 3.4 copy-done
  182.3 12.6 %shard_map.111 = bf16[1536,2048]{1,0:T(8,128)(2,1)S(1)} custom-call(s32[16,1,256]{2,1,0:T(1,128)S(1)} %bitcast.62, f32[16,1,256]{2,1,0:T(1,128)S(1)} %bitcast.64, bf16[2048,2048]{1,0:T(8,128)(2,1)S(1)} %copy-done, bf16[2048,2048]{1,0:T(8,128)(2,1)} %collective-permute-done.other_ref), custom_call_target="tpu_custom_call" | custom-call | flops 1610612736 | bytes 33554432 | tf_op jit(solution)/shard_map/pallas_call | solution.py:46
  194.9 0.0 slice-start.1
  194.9 9.0 %fusion.28 = f32[1536,640]{1,0:T(8,128)S(1)} fusion(bf16[1536,2048]{1,0:T(8,128)(2,1)S(1)} %shard_map.111, bf16[1,1408,2048]{2,1,0:T(8,128)(2,1)} %param.15), kind=kOutput, calls=%fused_computation.42 | convolution fusion | flops 4026531840 | bytes 12845056 | tf_op jit(solution)/shard_map/dot_general | solution.py:16
  203.9 0.0 collective-permute-done.1.other_ref
  203.9 12.1 %shard_map.112 = bf16[1536,2048]{1,0:T(8,128)(2,1)S(1)} custom-call(s32[16,1,256]{2,1,0:T(1,128)S(1)} %bitcast.63, f32[16,1,256]{2,1,0:T(1,128)S(1)} %bitcast.65, bf16[2048,2048]{1,0:T(8,128)(2,1)S(1)} %bitcast.61, bf16[2048,2048]{1,0:T(8,128)(2,1)} %collective-permute-done.1.other_ref), custom_call_target="tpu_custom_call" | custom-call | flops 1610612736 | bytes 33554432 | tf_op jit(solution)/shard_map/pallas_call | solution.py:46
  216.0 10.8 %multiply_convert_fusion.5 = (bf16[1536,640]{1,0:T(8,128)(2,1)}, bf16[1536,640]{1,0:T(8,128)(2,1)S(1)}, bf16[1536,640]{1,0:T(8,128)(2,1)S(1)}) fusion(bf16[32,48,640]{2,1,0:T(8,128)(2,1)S(1)} %copy-done.10, f32[1536,640]{1,0:T(8,128)S(1)} %fusion.28, bf16[1536,2048]{1,0:T(8,128)(2,1)S(1)} %shard_map.112, bf16[2048,1408]{1,0:T(8,128)(2,1)} %bitcast.79), kind=kOutput, calls=%fused_computation.33 | convolution fusion | flops 4042260480 | bytes 20709376 | tf_op jit(solution)/shard_map/dot_general | solution.py:16
  226.9 0.0 copy-done.2
  226.9 10.5 %multiply_convert_fusion.2 = bf16[2048,1280]{1,0:T(8,128)(2,1)} fusion(bf16[1536,2048]{1,0:T(8,128)(2,1)S(1)} %shard_map.112, bf16[1536,640]{1,0:T(8,128)(2,1)S(1)} %get-tuple-element.21.refs_2_, bf16[1536,640]{1,0:T(8,128)(2,1)S(1)} %get-tuple-element.19.refs_0_), kind=kOutput, calls=%fused_computation.3 | convolution fusion | flops 8066170880 | bytes 15466496 | tf_op jit(solution)/shard_map/dot_general | solution.py:16
  237.4 1.3 copy-done.4
  238.7 0.0 reduce-scatter.4.cloned.1.call-update
  238.7 3.2 slice.61
  241.9 5.5 %all-to-all-start.1 = ((bf16[32,48,768]{2,1,0:T(8,128)(2,1)}), bf16[32,48,768]{2,1,0:T(8,128)(2,1)}, u32[]{:S(2)}, u32[]{:S(2)}) async-start(bf16[32,48,768]{2,1,0:T(8,128)(2,1)} %slice.61), calls=%async_computation.1 | async-start | bytes 4718592 | tf_op jit(solution)/shard_map/all_to_all | solution.py:127
  247.4 0.0 reduce-scatter.6.cloned.1.call-start
  247.4 9.8 %fusion.23 = f32[1536,768]{1,0:T(8,128)} fusion(bf16[1536,2048]{1,0:T(8,128)(2,1)} %copy-done.1, bf16[1,1408,2048]{2,1,0:T(8,128)(2,1)} %param.15), kind=kOutput, calls=%fused_computation.37 | convolution fusion | flops 4831838208 | bytes 14155776 | tf_op jit(solution)/shard_map/dot_general | solution.py:16
  257.3 21.0 %all-to-all-done.1 = bf16[32,48,768]{2,1,0:T(8,128)(2,1)} async-done(((bf16[32,48,768]{2,1,0:T(8,128)(2,1)}), bf16[32,48,768]{2,1,0:T(8,128)(2,1)}, u32[]{:S(2)}, u32[]{:S(2)}) %all-to-all-start.1) | async-done | bytes 2359328 | tf_op jit(solution)/shard_map/all_to_all | solution.py:127
  278.2 11.8 %multiply_convert_fusion.3 = (bf16[1536,768]{1,0:T(8,128)(2,1)}, bf16[1536,768]{1,0:T(8,128)(2,1)S(1)}, bf16[1536,768]{1,0:T(8,128)(2,1)S(1)}) fusion(bf16[32,48,768]{2,1,0:T(8,128)(2,1)} %all-to-all-done.1, f32[1536,768]{1,0:T(8,128)} %fusion.23, bf16[1536,2048]{1,0:T(8,128)(2,1)} %copy-done.2, bf16[2048,1408]{1,0:T(8,128)(2,1)} %bitcast.80), kind=kOutput, calls=%fused_computation.19 | convolution fusion | flops 4850712576 | bytes 23592960 | tf_op jit(solution)/shard_map/dot_general | solution.py:16
  290.0 13.8 %multiply_convert_fusion = bf16[2048,1536]{1,0:T(8,128)(2,1)} fusion(bf16[1536,2048]{1,0:T(8,128)(2,1)} %copy-done.2, bf16[1536,768]{1,0:T(8,128)(2,1)S(1)} %get-tuple-element.22.refs_3_, bf16[1536,768]{1,0:T(8,128)(2,1)S(1)} %get-tuple-element.20.refs_1_), kind=kOutput, calls=%fused_computation.1 | convolution fusion | flops 9679405056 | bytes 17301504 | tf_op jit(solution)/shard_map/dot_general | solution.py:16
  303.9 1.5 copy-done.6
  305.3 1.4 copy-done.8
  306.7 0.0 reduce-scatter.6.cloned.1.call-update
  306.7 0.0 reduce-scatter.8.cloned.1.call-start
  306.8 14.4 %multiply_convert_fusion.1 = bf16[1408,2048]{1,0:T(8,128)(2,1)} fusion(bf16[1536,2048]{1,0:T(8,128)(2,1)} %copy-done.1, bf16[1536,768]{1,0:T(8,128)(2,1)} %get-tuple-element.26, bf16[1536,640]{1,0:T(8,128)(2,1)} %get-tuple-element.29), kind=kOutput, calls=%fused_computation.2 | convolution fusion | flops 8872787968 | bytes 16384000 | tf_op jit(solution)/shard_map/dot_general | solution.py:16
  321.2 0.0 reduce-scatter.8.cloned.1.call-update
  321.3 0.0 copy-start.3
  321.3 2.7 copy-done.3
  324.0 1.5 copy-done.5
  325.5 1.7 copy-done.7
  327.2 1.8 copy-done.9
  328.9 24.3 %shard_map.113 = bf16[1536,2048]{1,0:T(8,128)(2,1)} custom-call(bf16[1536,640]{1,0:T(8,128)(2,1)S(1)} %get-tuple-element.19.refs_0_, bf16[1536,768]{1,0:T(8,128)(2,1)S(1)} %copy-done.7, bf16[1536,640]{1,0:T(8,128)(2,1)S(1)} %copy-done.5, bf16[1536,768]{1,0:T(8,128)(2,1)S(1)} %copy-done.9, bf16[2048,1408]{1,0:T(8,128)(2,1)S(1)} %bitcast.66, ...), custom_call_target="tpu_custom_call" | custom-call | flops 17716740096 | bytes 11534336 | tf_op jit(solution)/shard_map/pallas_call | solution.py:74
  353.2 80.1 %all_to_all.16 = bf16[32,48,2048]{2,1,0:T(8,128)(2,1)S(1)} all-to-all(bf16[32,48,2048]{2,1,0:T(8,128)(2,1)} %bitcast.69), channel_id=1, replica_groups=mesh['dp'=4,'expert'=32] {'expert'}, dimensions={0} | all-to-all | bytes 12582912 | tf_op jit(solution)/shard_map/all_to_all | solution.py:166
  433.3 1.9 fusion.31
  435.2 1.4 fusion.41
  436.6 0.0 reduce-scatter.6.cloned.1.call-done
  436.6 1.5 fusion.40
  438.1 1.2 maximum_bitcast_fusion
  439.3 1.2 maximum_bitcast_fusion.1
  (31 shorter events, 0.2 us)
Async XLA Ops:
  7.2 98.1 %all-gather.5.cloned.1.call-start = ((), (), s32[]{:S(2)}) async-start(), calls=%async_computation.6 | async-start | bytes 8912896 | tf_op jit(solution)/shard_map/all_gather | solution.py:102
  7.9 169.9 %all-gather.7.cloned.1.call-start = ((), (), s32[]{:S(2)}) async-start(), calls=%async_computation.7 | async-start | bytes 8912896 | tf_op jit(solution)/shard_map/all_gather | solution.py:103
  8.6 8.1 %copy-start.11 = (s32[128,6]{0,1:T(8,128)S(1)}, s32[128,6]{0,1:T(8,128)}, u32[]{:S(2)}) copy-start(s32[128,6]{0,1:T(8,128)} %param.12) | copy-start | bytes 9220
  8.7 8.1 %copy-start.12 = (f32[128,6]{0,1:T(8,128)S(1)}, f32[128,6]{0,1:T(8,128)}, u32[]{:S(2)}) copy-start(f32[128,6]{0,1:T(8,128)} %param.11) | copy-start | bytes 9220
  8.7 426.5 %reduce-scatter.4.cloned.1.call-start = ((), (), s32[]{:S(2)}) async-start(), calls=%async_computation.8 | async-start | bytes 6553600 | tf_op jit(solution)/shard_map/reduce_scatter | solution.py:158
  105.2 73.7 %collective-permute-start = (bf16[2048,2048]{1,0:T(8,128)(2,1)}, bf16[2048,2048]{1,0:T(8,128)(2,1)}, u32[]{:S(2)}, u32[]{:S(2)}) collective-permute-start(bf16[2048,2048]{1,0:T(8,128)(2,1)} %all-gather.5.cloned.1.call-done.own_ref), channel_id=1, source_target_pairs={{0,1},{1,0},{2,3},{3,2},{4,5},{5,4},{6,7},{7,6},{8,9},{9,8},{10,11... | collective-permute-start | bytes 25165832 | tf_op jit(solution)/shard_map/ppermute | solution.py:131
  177.8 26.1 %collective-permute-start.1 = (bf16[2048,2048]{1,0:T(8,128)(2,1)}, bf16[2048,2048]{1,0:T(8,128)(2,1)}, u32[]{:S(2)}, u32[]{:S(2)}) collective-permute-start(bf16[2048,2048]{1,0:T(8,128)(2,1)} %all-gather.7.cloned.1.call-done.own_ref), channel_id=1, source_target_pairs={{0,1},{1,0},{2,3},{3,2},{4,5},{5,4},{6,7},{7,6},{8,9},{9,8},{10,11... | collective-permute-start | bytes 25165832 | tf_op jit(solution)/shard_map/ppermute | solution.py:132
  178.9 3.4 copy-start
  182.3 21.6 %slice-start = ((s8[8388608]{0:T(1024)(128)(4,1)}), s8[4194304]{0:T(1024)(128)(4,1)S(1)}, s32[]{:S(2)}) async-start(s8[8388608]{0:T(1024)(128)(4,1)} %bitcast.60), calls=%async_computation.11 | async-start | bytes 8388608
  194.9 9.0 %copy-start.1 = (bf16[1536,2048]{1,0:T(8,128)(2,1)}, bf16[1536,2048]{1,0:T(8,128)(2,1)S(1)}, u32[]{:S(2)}) copy-start(bf16[1536,2048]{1,0:T(8,128)(2,1)S(1)} %shard_map.111) | copy-start | bytes 18874372
  194.9 9.0 %slice-start.1 = ((s8[8388608]{0:T(1024)(128)(4,1)}), s8[4194304]{0:T(1024)(128)(4,1)S(1)}, s32[]{:S(2)}) async-start(s8[8388608]{0:T(1024)(128)(4,1)} %bitcast.60), calls=%async_computation.12 | async-start | bytes 8388608
  203.9 12.2 %copy-start.10 = (bf16[32,48,640]{2,1,0:T(8,128)(2,1)S(1)}, bf16[32,48,640]{2,1,0:T(8,128)(2,1)}, u32[]{:S(2)}) copy-start(bf16[32,48,640]{2,1,0:T(8,128)(2,1)} %all_to_all.15) | copy-start | bytes 5898244
  216.0 10.9 %copy-start.2 = (bf16[1536,2048]{1,0:T(8,128)(2,1)}, bf16[1536,2048]{1,0:T(8,128)(2,1)S(1)}, u32[]{:S(2)}) copy-start(bf16[1536,2048]{1,0:T(8,128)(2,1)S(1)} %shard_map.112) | copy-start | bytes 18874372
  237.4 1.3 copy-start.4
  241.9 36.3 %all-to-all-start.1 = ((bf16[32,48,768]{2,1,0:T(8,128)(2,1)}), bf16[32,48,768]{2,1,0:T(8,128)(2,1)}, u32[]{:S(2)}, u32[]{:S(2)}) async-start(bf16[32,48,768]{2,1,0:T(8,128)(2,1)} %slice.61), calls=%async_computation.1 | async-start | bytes 4718592 | tf_op jit(solution)/shard_map/all_to_all | solution.py:127
  247.4 189.2 %reduce-scatter.6.cloned.1.call-start = ((), (), s32[]{:S(2)}) async-start(), calls=%async_computation.9 | async-start | bytes 7864320 | tf_op jit(solution)/shard_map/reduce_scatter | solution.py:158
  303.9 1.5 copy-start.6
  305.3 1.4 copy-start.8
  306.7 133.8 %reduce-scatter.8.cloned.1.call-start = ((), (), s32[]{:S(2)}) async-start(), calls=%async_computation.10 | async-start | bytes 7208960 | tf_op jit(solution)/shard_map/reduce_scatter | solution.py:163
  321.3 2.7 copy-start.3
  324.0 1.5 copy-start.5
  325.5 1.7 copy-start.7
  327.2 1.8 copy-start.9
Sparse Core Ops, SparseCore 0:
  10.1 95.0 all-gather.4
  107.4 70.3 all-gather.6
  238.8 54.8 reduce-scatter.3
  306.9 63.0 reduce-scatter.5
  372.8 59.4 reduce-scatter.7
